TPU v7x, 512 devices: a whole 4x8x8 slice. The times are simulated.
512 devices in a mesh: tm: 64 (over z_lo, y, core), space: 8 (over z_hi, x).
Axes of the slice: x: 4, y: 8, z: 8 (z_hi: 2, z_lo: 4; z = z_hi * 4 + z_lo), core: 2. Of those that a mesh axis runs over, the one named last changes fastest.
Arguments:
- queries: bfloat16 [196608, 512], P(('tm', 'space'))
- keys: bfloat16 [196608, 512], P(('tm', 'space'))
- values: bfloat16 [196608, 512], P(('tm', 'space')), may hold values from -6 to 6
- block_mask: int32 [1536, 6, 3], P(('tm', 'space')), may hold values 0 or 1
- tile_counts: int32 [64, 8], P('tm', 'space'), may hold values from 193 to 384, as said below
Outputs:
- attended: bfloat16 [196608, 512], P(('tm', 'space'))
Inputs may be any that keep to these rules, and one draw needn't show every extreme that they name: `tile_counts`: at least one tile has all 384 slots live.
All inputs are finite; a program needn't handle non-finite values. No bound on the sum of `block_mask` on one device may be relied on, other than what follows from the above.
Results may differ from a plain program's by a relative error of at most 0.0049.
Values may be sent and summed in bfloat16 or wider, within the bound.
No kernel may reach another device: no remote copies, remote signals or barrier semaphores. Data moves between devices by JAX's collectives and lax.ppermute only.
A program may use at most 128 MiB of HBM per device.

v0:
```python
import jax
import jax.numpy as jnp
from jax import lax
from jax.sharding import PartitionSpec as P

HEAD = 128
BLK = 128


def with_halo(block, sides, width):
    for axis, dim in sides:
        count = lax.axis_size(axis)
        forward = [(i, i + 1) for i in range(count - 1)]
        backward = [(target, source) for source, target in forward]
        low = lax.ppermute(
            lax.slice_in_dim(block, block.shape[dim] - width, None, axis=dim), axis, forward
        )
        high = lax.ppermute(lax.slice_in_dim(block, 0, width, axis=dim), axis, backward)
        block = jnp.concatenate([low, block, high], axis=dim)
    return block


def from_partner(value, axis, bit):
    mask = 2**bit
    pairs = [(source, source ^ mask) for source in range(lax.axis_size(axis))]
    return lax.ppermute(value, axis, pairs)


def per_device(queries, keys, values, block_mask, tile_counts):
    tok_rows = queries.shape[0]
    width = queries.shape[1]
    heads = width // HEAD
    scale = 1.0 / HEAD**0.5
    tm_index = lax.axis_index("tm")
    space_index = lax.axis_index("space")
    space_size = lax.axis_size("space")
    tm_size = lax.axis_size("tm")
    bit_count = tm_size.bit_length() - 1
    counts_every = lax.all_gather(tile_counts.reshape(1), ("tm", "space"), axis=0, tiled=True)
    row_ids = jnp.arange(tok_rows, dtype=jnp.int32)
    key_value = jnp.concatenate([keys, values], axis=1)
    band_rows = with_halo(key_value, (("space", 0),), tok_rows)
    own_flat = tm_index * space_size + space_index
    own_count = counts_every[own_flat]
    lower_count = jnp.where(space_index > 0, counts_every[jnp.maximum(own_flat - 1, 0)], 0)
    upper_count = jnp.where(
        space_index < space_size - 1,
        counts_every[jnp.minimum(own_flat + 1, tm_size * space_size - 1)],
        0,
    )
    band_valid = []
    for neighbour_count in (lower_count, own_count, upper_count):
        live = row_ids < neighbour_count
        band_valid.append(jnp.broadcast_to(live[None, :], (tok_rows, tok_rows)))
    piece_rows = [band_rows]
    piece_valid = [jnp.concatenate(band_valid, axis=1)]
    for bit_number in range(bit_count):
        partner = jnp.bitwise_xor(tm_index, 1 << bit_number)
        partner_count = counts_every[partner * space_size + space_index]
        blocks = jnp.repeat(jnp.repeat(block_mask[:, bit_number, :], BLK, axis=0), BLK, axis=1)
        piece_valid.append((blocks == 1) & (row_ids < partner_count)[None, :])
        piece_rows.append(from_partner(key_value, "tm", bit_number))
    query_heads = queries.reshape(tok_rows, heads, HEAD)
    all_rows = jnp.concatenate(piece_rows, axis=0)
    valid = jnp.concatenate(piece_valid, axis=1)
    key_heads = all_rows[:, :width].reshape(-1, heads, HEAD)
    scores = (
        jnp.einsum("qhe,khe->hqk", query_heads, key_heads, preferred_element_type=jnp.float32)
        * scale
    )
    scores = jnp.where(valid[None], scores, jnp.float32(-1e30))
    top = jnp.max(scores, axis=2, keepdims=True)
    expo = jnp.where(valid[None], jnp.exp(scores - top), jnp.float32(0.0))
    probs = (expo / jnp.sum(expo, axis=2, keepdims=True)).astype(jnp.bfloat16)
    value_heads = all_rows[:, width:].reshape(-1, heads, HEAD)
    result = jnp.einsum("hqk,khe->qhe", probs, value_heads, preferred_element_type=jnp.float32)
    result = result.reshape(tok_rows, width)
    result = jnp.where((row_ids < own_count)[:, None], result, jnp.float32(0.0))
    return result.astype(jnp.bfloat16)


def solution(mesh):
    placed = (
        P(("tm", "space"), None),
        P(("tm", "space"), None),
        P(("tm", "space"), None),
        P(("tm", "space"), None, None),
        P("tm", "space"),
    )
    return jax.shard_map(
        per_device, mesh=mesh, in_specs=placed, out_specs=P(("tm", "space"), None), check_vma=False
    )
```

profile of v0, /device:TPU:26, one launch (start us, length us, event | category | flops | bytes accessed | tf_op | source)
XLA Modules:
  0.0 258.8 jit_solution(11348115405881292565)
XLA Ops:
  0.0 1.3 copy.16
  1.3 1.2 copy.17
  2.6 2.2 collective-permute-start.4
  4.8 2.4 collective-permute-start.3
  7.2 1.9 collective-permute-start.2
  9.1 7.8 %collective-permute-start.1 = (bf16[384,1024]{0,1:T(8,128)(2,1)S(1)}, bf16[384,1024]{0,1:T(8,128)(2,1)}, u32[]{:S(2)}, u32[]{:S(2)}) collective-permute-start(bf16[384,1024]{0,1:T(8,128)(2,1)S(1)} %pad_maximum_fusion), channel_id=1, source_target_pairs={{1,0},{2,1},{3,2},{4,3},{5,4},{6,5},{7,6},{9,8},{10,9},{11,10},{12... | collective-permute-start | bytes 2359304 | tf_op jit(solution)/shard_map/ppermute | solution.py:18
  16.9 1.9 collective-permute-start
  19.6 127.8 %all-reduce = s32[512]{0:T(512)S(1)} all-reduce(s32[512]{0:T(512)S(1)} %bitcast_dynamic-update-slice_fusion), channel_id=2, replica_groups=mesh['tm'=64,'space'=8] {'tm','space'}, use_global_device_ids=true, to_apply=%add | all-reduce | flops 512 | bytes 4096
  150.3 1.1 iota_compare_fusion.8
  151.5 1.6 slice_compare_fusion
  153.0 1.4 copy.33
  154.4 1.3 copy.32
  157.5 1.2 broadcast_bitcast_fusion.3
  158.7 1.3 broadcast_bitcast_fusion.2
  160.0 1.4 broadcast_dynamic-update-slice_fusion.2
  161.4 1.4 broadcast_dynamic-update-slice_fusion.1
  162.8 1.4 broadcast_dynamic-update-slice_fusion
  164.2 1.1 iota_compare_fusion.1
  171.5 0.8 constant_dynamic-update-slice_fusion.13
  173.9 1.4 constant_dynamic-update-slice_fusion.10
  176.7 5.9 %collective-permute-start.5 = (bf16[384,1024]{0,1:T(8,128)(2,1)S(1)}, bf16[384,1024]{0,1:T(8,128)(2,1)S(1)}, u32[]{:S(2)}, u32[]{:S(2)}) collective-permute-start(bf16[384,1024]{0,1:T(8,128)(2,1)S(1)} %pad_maximum_fusion), channel_id=1, source_target_pairs={{0,64},{8,72},{16,80},{24,88},{32,96},{40,104},{48,112},{56,120},{... | collective-permute-start | bytes 2359304 | tf_op jit(solution)/shard_map/ppermute | solution.py:26
  182.7 1.2 constant_dynamic-update-slice_fusion.8
  183.9 3.6 %collective-permute-start.6 = (bf16[384,1024]{0,1:T(8,128)(2,1)S(1)}, bf16[384,1024]{0,1:T(8,128)(2,1)S(1)}, u32[]{:S(2)}, u32[]{:S(2)}) collective-permute-start(bf16[384,1024]{0,1:T(8,128)(2,1)S(1)} %pad_maximum_fusion), channel_id=1, source_target_pairs={{0,128},{8,136},{16,144},{24,152},{32,160},{40,168},{48,176},{56,1... | collective-permute-start | bytes 2359304 | tf_op jit(solution)/shard_map/ppermute | solution.py:26
  187.7 2.1 collective-permute-start.7
  189.8 1.3 constant_dynamic-update-slice_fusion.6
  191.1 1.3 constant_dynamic-update-slice_fusion.5
  192.7 26.3 %collective-permute-done.5 = bf16[384,1024]{0,1:T(8,128)(2,1)S(1)} collective-permute-done((bf16[384,1024]{0,1:T(8,128)(2,1)S(1)}, bf16[384,1024]{0,1:T(8,128)(2,1)S(1)}, u32[]{:S(2)}, u32[]{:S(2)}) %collective-permute-start.5) | collective-permute-done | bytes 786464 | tf_op jit(solution)/shard_map/ppermute | solution.py:26
  219.4 6.3 %collective-permute-done.7 = bf16[384,1024]{0,1:T(8,128)(2,1)S(1)} collective-permute-done((bf16[384,1024]{0,1:T(8,128)(2,1)S(1)}, bf16[384,1024]{0,1:T(8,128)(2,1)S(1)}, u32[]{:S(2)}, u32[]{:S(2)}) %collective-permute-start.7) | collective-permute-done | bytes 786464 | tf_op jit(solution)/shard_map/ppermute | solution.py:26
  225.9 3.4 %fusion.21 = (bf16[3456,512]{0,1:T(8,128)(2,1)}, bf16[3456,512]{0,1:T(8,128)(2,1)}) fusion(bf16[3456,1024]{0,1:T(8,128)(2,1)S(1)} %constant_dynamic-update-slice_fusion), kind=kLoop, calls=%fused_computation.71 | loop fusion | bytes 14155776 | tf_op jit(solution)/shard_map/slice | solution.py:66
  229.3 18.2 %fusion.23 = (f32[4,384]{1,0:T(4,128)S(1)}, f32[4,384,3456]{1,2,0:T(8,128)}) fusion(pred[384,3456]{0,1:T(8,128)(4,1)} %constant_dynamic-update-slice_fusion.9, bf16[3456,4,128]{0,2,1:T(8,128)(2,1)} %bitcast.112, bf16[384,512]{1,0:T(8,128)(2,1)S(1)} %copy-done), kind=kOutput, calls=%fused_computation.73 | convolution fusion | flops 1385500032 | bytes 26499072 | tf_op jit(solution)/shard_map/sub | solution.py:73
  247.5 10.2 %fusion.5 = bf16[4,128,384]{2,1,0:T(8,128)(2,1)S(1)} fusion(bf16[3456,4,128]{0,2,1:T(8,128)(2,1)} %bitcast.111, f32[4,384,3456]{1,2,0:T(8,128)} %get-tuple-element.23, f32[4,384]{1,0:T(4,128)S(1)} %get-tuple-element.22), kind=kOutput, calls=%fused_computation.8 | convolution fusion | flops 1369571328 | bytes 25171968 | tf_op jit(solution)/shard_map/hqk,khe->qhe/dot_general | solution.py:76
  257.9 0.9 select_convert_fusion
  (46 shorter events, 13.9 us)
Async XLA Ops:
  0.0 229.3 %copy-start = (bf16[384,512]{1,0:T(8,128)(2,1)S(1)}, bf16[384,512]{1,0:T(8,128)(2,1)}, u32[]{:S(2)}) copy-start(bf16[384,512]{1,0:T(8,128)(2,1)} %param.5) | copy-start | bytes 1179652
  2.6 190.0 %collective-permute-start.4 = (bf16[384,1024]{0,1:T(8,128)(2,1)S(1)}, bf16[384,1024]{0,1:T(8,128)(2,1)S(1)}, u32[]{:S(2)}, u32[]{:S(2)}) collective-permute-start(bf16[384,1024]{0,1:T(8,128)(2,1)S(1)} %pad_maximum_fusion), channel_id=1, source_target_pairs={{0,32},{8,40},{16,48},{24,56},{32,0},{40,8},{48,16},{56,24},{64,96... | collective-permute-start | bytes 2359304 | tf_op jit(solution)/shard_map/ppermute | solution.py:26
  4.8 187.5 %collective-permute-start.3 = (bf16[384,1024]{0,1:T(8,128)(2,1)S(1)}, bf16[384,1024]{0,1:T(8,128)(2,1)S(1)}, u32[]{:S(2)}, u32[]{:S(2)}) collective-permute-start(bf16[384,1024]{0,1:T(8,128)(2,1)S(1)} %pad_maximum_fusion), channel_id=1, source_target_pairs={{0,16},{8,24},{16,0},{24,8},{32,48},{40,56},{48,32},{56,40},{64,80... | collective-permute-start | bytes 2359304 | tf_op jit(solution)/shard_map/ppermute | solution.py:26
  7.2 176.7 %collective-permute-start.2 = (bf16[384,1024]{0,1:T(8,128)(2,1)S(1)}, bf16[384,1024]{0,1:T(8,128)(2,1)}, u32[]{:S(2)}, u32[]{:S(2)}) collective-permute-start(bf16[384,1024]{0,1:T(8,128)(2,1)S(1)} %pad_maximum_fusion), channel_id=1, source_target_pairs={{0,8},{8,0},{16,24},{24,16},{32,40},{40,32},{48,56},{56,48},{64,72... | collective-permute-start | bytes 2359304 | tf_op jit(solution)/shard_map/ppermute | solution.py:26
  9.1 178.5 %collective-permute-start.1 = (bf16[384,1024]{0,1:T(8,128)(2,1)S(1)}, bf16[384,1024]{0,1:T(8,128)(2,1)}, u32[]{:S(2)}, u32[]{:S(2)}) collective-permute-start(bf16[384,1024]{0,1:T(8,128)(2,1)S(1)} %pad_maximum_fusion), channel_id=1, source_target_pairs={{1,0},{2,1},{3,2},{4,3},{5,4},{6,5},{7,6},{9,8},{10,9},{11,10},{12... | collective-permute-start | bytes 2359304 | tf_op jit(solution)/shard_map/ppermute | solution.py:18
  16.9 159.8 %collective-permute-start = (bf16[384,1024]{0,1:T(8,128)(2,1)S(1)}, bf16[384,1024]{0,1:T(8,128)(2,1)}, u32[]{:S(2)}, u32[]{:S(2)}) collective-permute-start(bf16[384,1024]{0,1:T(8,128)(2,1)S(1)} %pad_maximum_fusion), channel_id=1, source_target_pairs={{0,1},{1,2},{2,3},{3,4},{4,5},{5,6},{6,7},{8,9},{9,10},{10,11},{11... | collective-permute-start | bytes 2359304 | tf_op jit(solution)/shard_map/ppermute | solution.py:15
  176.7 42.3 %collective-permute-start.5 = (bf16[384,1024]{0,1:T(8,128)(2,1)S(1)}, bf16[384,1024]{0,1:T(8,128)(2,1)S(1)}, u32[]{:S(2)}, u32[]{:S(2)}) collective-permute-start(bf16[384,1024]{0,1:T(8,128)(2,1)S(1)} %pad_maximum_fusion), channel_id=1, source_target_pairs={{0,64},{8,72},{16,80},{24,88},{32,96},{40,104},{48,112},{56,120},{... | collective-permute-start | bytes 2359304 | tf_op jit(solution)/shard_map/ppermute | solution.py:26
  183.9 35.3 %collective-permute-start.6 = (bf16[384,1024]{0,1:T(8,128)(2,1)S(1)}, bf16[384,1024]{0,1:T(8,128)(2,1)S(1)}, u32[]{:S(2)}, u32[]{:S(2)}) collective-permute-start(bf16[384,1024]{0,1:T(8,128)(2,1)S(1)} %pad_maximum_fusion), channel_id=1, source_target_pairs={{0,128},{8,136},{16,144},{24,152},{32,160},{40,168},{48,176},{56,1... | collective-permute-start | bytes 2359304 | tf_op jit(solution)/shard_map/ppermute | solution.py:26
  187.7 38.1 %collective-permute-start.7 = (bf16[384,1024]{0,1:T(8,128)(2,1)S(1)}, bf16[384,1024]{0,1:T(8,128)(2,1)S(1)}, u32[]{:S(2)}, u32[]{:S(2)}) collective-permute-start(bf16[384,1024]{0,1:T(8,128)(2,1)S(1)} %pad_maximum_fusion), channel_id=1, source_target_pairs={{0,256},{8,264},{16,272},{24,280},{32,288},{40,296},{48,304},{56,3... | collective-permute-start | bytes 2359304 | tf_op jit(solution)/shard_map/ppermute | solution.py:26
  247.5 10.4 %copy-start.1 = (pred[384]{0:T(512)(128)(4,1)S(1)}, pred[384]{0:T(512)(128)(4,1)}, u32[]{:S(2)}) copy-start(pred[384]{0:T(512)(128)(4,1)} %iota_compare_fusion.8) | copy-start | bytes 1156
where the time goes:
time: 260 us; the launch traced here: 259 us
  blocking collectives  128 us (49%)
  waiting for transfers between devices  32.7 us (13%)
  matrix products  28.4 us (11%)
  starting transfers between devices  27.9 us (11%)
  local copies, waits for them, and re-layouts  25.3 us (10%)
  other arithmetic  14.6 us (6%)
    unnamed x1, blocking collectives  128 us
    ppermute x6, waiting for transfers between devices, from_partner(): return lax.ppermute(value, axis, pairs)  32.7 us
    sub x1, matrix products, per_device(): expo = jnp.where(valid[None], jnp.exp(scores - top), jnp.float32(0.0))  18.2 us
    ppermute x6, starting transfers between devices, from_partner(): return lax.ppermute(value, axis, pairs)  18.1 us
    unnamed x31, local copies, waits for them, and re-layouts  17.3 us
    dot_general x1, matrix products, per_device(): jnp.einsum('hqk,khe->qhe', probs, value_heads, preferred_element_type=jnp...  10.2 us
    ppermute x1, starting transfers between devices, with_halo(): lax.ppermute(lax.slice_in_dim(block, 0, width, axis=dim), axis, backward)  7.82 us
  transfers between devices with their start and end apart: 8, of which 2 were waited for; matrix products, arithmetic and copies ran while one was open for 13% of the time, Pallas kernels for 0%

commit v1 on v0

v1 whole, which is shorter than its diff:
```python
import functools

import jax
import jax.numpy as jnp
from jax import lax
from jax.experimental import pallas as pl
from jax.experimental.pallas import tpu as pltpu
from jax.sharding import PartitionSpec as P

HEAD = 128
BLK = 128
LOG2E = 1.4426950408889634
NEG = -1e30


def attend_kernel(kinds, packed, first, last, heads, scal, q_ref, *refs):
    refs = list(refs)
    tiles = []
    width = heads * HEAD
    for whole in packed:
        if whole:
            kv = refs.pop(0)
            tiles.append((kv, kv, width))
        else:
            tiles.append((refs.pop(0), refs.pop(0), 0))
    if not first:
        m_in, l_in, a_in = refs[:3]
        refs = refs[3:]
    if last:
        (out_ref,) = refs
    else:
        m_out, l_out, a_out = refs
    rows = q_ref.shape[0]
    blocks = rows // BLK
    scale = (1.0 / HEAD**0.5) * LOG2E
    lane = lax.broadcasted_iota(jnp.int32, (1, BLK), 1).astype(jnp.float32)

    valid = []
    for kind, (k_ref, _, _) in zip(kinds, tiles):
        if kind == "own":
            count = jnp.full((1, BLK), scal[0], jnp.int32).astype(jnp.float32)
        else:
            tail = k_ref[rows - 16 : rows, 0 : 3 * BLK].astype(jnp.float32)[15:16]
            count = jnp.where(
                tail[:, :BLK] == jnp.inf,
                tail[:, BLK : 2 * BLK] * 128.0 + tail[:, 2 * BLK :],
                jnp.float32(rows),
            )
        per_q = []
        for qb in range(blocks):
            if kind == "own":
                gates = [None] * blocks
            elif kind == "low":
                gates = [scal[1]] * blocks
            elif kind == "high":
                gates = [scal[2]] * blocks
            else:
                base = 3 + (qb * 6 + kind) * blocks
                gates = [scal[base + kb] for kb in range(blocks)]
            row = []
            for kb in range(blocks):
                limit = count - float(kb * BLK)
                if gates[kb] is not None:
                    limit = jnp.where(gates[kb] == 1, limit, jnp.float32(-1.0))
                row.append(jnp.broadcast_to(lane < limit, (BLK, BLK)))
            per_q.append(row)
            if kind in ("own", "low", "high"):
                per_q = [row] * blocks
                break
        valid.append(per_q)

    for h in range(heads):
        hs = slice(h * HEAD, (h + 1) * HEAD)
        q = q_ref[:, hs]
        scores = []
        top = None
        for t, (k_ref, _, _) in enumerate(tiles):
            s = lax.dot_general(
                q, k_ref[:, hs], (((1,), (1,)), ((), ())), preferred_element_type=jnp.float32
            )
            cols = []
            for kb in range(blocks):
                col = jnp.concatenate(
                    [
                        jnp.where(
                            valid[t][qb][kb],
                            s[qb * BLK : (qb + 1) * BLK, kb * BLK : (kb + 1) * BLK],
                            jnp.float32(NEG),
                        )
                        for qb in range(blocks)
                    ],
                    axis=0,
                )
                cols.append(col)
                top = col if top is None else jnp.maximum(top, col)
            scores.append(cols)
        top = jnp.broadcast_to(jnp.max(top, axis=1, keepdims=True), (rows, HEAD))
        if not first:
            m_old = m_in[:, hs]
            top = jnp.maximum(top, m_old)
        top_s = top * scale
        total = None
        acc = None
        if not first:
            alpha = jnp.exp2(m_old * scale - top_s)
            total = l_in[:, hs] * alpha
            acc = a_in[:, hs] * alpha
        for t, (_, v_ref, v_off) in enumerate(tiles):
            probs = []
            for kb in range(blocks):
                p = jnp.exp2(scores[t][kb] * scale - top_s)
                total = p if total is None else total + p
                probs.append(p.astype(jnp.bfloat16))
            part = jnp.dot(
                jnp.concatenate(probs, axis=1),
                v_ref[:, v_off + h * HEAD : v_off + (h + 1) * HEAD],
                preferred_element_type=jnp.float32,
            )
            acc = part if acc is None else acc + part
        if last:
            norm = 1.0 / jnp.sum(total, axis=1, keepdims=True)
            live = lax.broadcasted_iota(jnp.int32, (rows, HEAD), 0) < scal[0]
            out_ref[:, hs] = jnp.where(live, acc * norm, 0.0).astype(out_ref.dtype)
        else:
            m_out[:, hs] = top
            l_out[:, hs] = total
            a_out[:, hs] = acc


def attend(scal, q, tiles, state, last):
    rows, width = q.shape
    heads = width // HEAD
    kinds = tuple(t[0] for t in tiles)
    packed = tuple(len(t) == 2 for t in tiles)
    arrays = [a for t in tiles for a in t[1:]]
    first = state is None
    ins = [scal, q] + arrays + ([] if first else list(state))
    vmem = pl.BlockSpec(memory_space=pltpu.VMEM)
    shape = (rows, width)
    if last:
        out_shape = jax.ShapeDtypeStruct(shape, jnp.bfloat16)
        out_specs = vmem
    else:
        out_shape = [jax.ShapeDtypeStruct(shape, jnp.float32)] * 3
        out_specs = [vmem] * 3
    pairs = rows * rows * heads * len(tiles)
    return pl.pallas_call(
        functools.partial(attend_kernel, kinds, packed, first, last, heads),
        out_shape=out_shape,
        in_specs=[pl.BlockSpec(memory_space=pltpu.SMEM)] + [vmem] * (len(ins) - 1),
        out_specs=out_specs,
        compiler_params=pltpu.CompilerParams(vmem_limit_bytes=40 << 20),
        cost_estimate=pl.CostEstimate(
            flops=4 * pairs * HEAD, transcendentals=pairs, bytes_accessed=len(ins) * 2 * rows * width
        ),
        name="attend_" + "_".join(str(k) for k in kinds),
    )(*ins)


def after(value, *earlier):
    return lax.optimization_barrier((value,) + earlier)[0]


def per_device(queries, keys, values, block_mask, tile_counts):
    rows, width = queries.shape
    tm_size = lax.axis_size("tm")
    space_size = lax.axis_size("space")
    space_index = lax.axis_index("space")
    count = tile_counts.reshape(())

    def partner(value, mask):
        return lax.ppermute(value, "tm", [(i, i ^ mask) for i in range(tm_size)])

    scal = jnp.concatenate(
        [
            jnp.stack(
                [
                    count,
                    (space_index > 0).astype(jnp.int32),
                    (space_index < space_size - 1).astype(jnp.int32),
                ]
            ),
            block_mask.reshape(-1),
        ]
    )
    column = lax.broadcasted_iota(jnp.int32, (rows, width), 1) // HEAD
    row = lax.broadcasted_iota(jnp.int32, (rows, width), 0)
    code = jnp.where(
        column == 0,
        jnp.float32(jnp.inf),
        jnp.where(column == 1, count >> 7, count & 127).astype(jnp.float32),
    ).astype(jnp.bfloat16)
    marked = jnp.where((row == rows - 1) & (count < rows), code, keys)

    up = [(i, i + 1) for i in range(space_size - 1)]
    down = [(i + 1, i) for i in range(space_size - 1)]
    y2_k = partner(marked, 4)
    y1_k = partner(marked, 2)
    both = jnp.concatenate([marked, values], axis=1)
    low = lax.ppermute(both, "space", up)
    high = lax.ppermute(both, "space", down)
    z1 = partner(both, 16)
    y4_k = partner(y2_k, 12)
    y2_v = partner(after(values, y2_k, y1_k), 4)
    z2 = partner(after(both, y2_k), 32)
    y4_v = partner(after(y2_v, y4_k), 12)
    y1_v = partner(after(values, y2_v, y4_k), 2)
    core = partner(after(both, y2_k), 1)

    state = attend(scal, queries, [("own", marked, values), (0, core)], None, False)
    state = attend(
        scal,
        queries,
        [("low", low), ("high", high), (4, z1), (2, y2_k, y2_v)],
        state,
        False,
    )
    return attend(
        scal, queries, [(5, z2), (1, y1_k, y1_v), (3, y4_k, y4_v)], state, True
    )


def solution(mesh):
    placed = (
        P(("tm", "space"), None),
        P(("tm", "space"), None),
        P(("tm", "space"), None),
        P(("tm", "space"), None, None),
        P("tm", "space"),
    )
    return jax.shard_map(
        per_device, mesh=mesh, in_specs=placed, out_specs=P(("tm", "space"), None), check_vma=False
    )
```

time: 260 us -> 133 us (0.51)
  the two profiles are of different devices: /device:TPU:26 before, /device:TPU:256 now
where the time goes in v1:
time: 133 us; the launch traced here: 132 us
  waiting for transfers between devices  62.8 us (47%)
  starting transfers between devices  47.3 us (36%)
  Pallas kernels  14.5 us (11%)
  local copies, waits for them, and re-layouts  3.64 us (3%)
  other arithmetic  3.21 us (2%)
    ppermute x9, waiting for transfers between devices, partner(): return lax.ppermute(value, 'tm', [(i, i ^ mask) for i in range(tm_size)])  62.8 us
    ppermute x9, starting transfers between devices, partner(): return lax.ppermute(value, 'tm', [(i, i ^ mask) for i in range(tm_size)])  35.4 us
    pallas_call x3, Pallas kernels, attend(): pl.pallas_call(functools.partial(attend_kernel, kinds, packed, first, las...  14.5 us
    ppermute x1, starting transfers between devices, per_device(): high = lax.ppermute(both, 'space', down)  8.46 us
    unnamed x15, local copies, waits for them, and re-layouts  3.56 us
    ppermute x1, starting transfers between devices, per_device(): low = lax.ppermute(both, 'space', up)  3.39 us
  transfers between devices with their start and end apart: 11, of which 4 were waited for; matrix products, arithmetic and copies ran while one was open for 2% of the time, Pallas kernels for 7%

profile of v1, /device:TPU:256, one launch (start us, length us, event | category | flops | bytes accessed | tf_op | source)
XLA Modules:
  0.0 132.3 jit_solution(16622623071436676243)
XLA Ops:
  0.7 1.1 fusion.refs_0_
  1.8 0.0 copy-start
  1.8 4.6 %collective-permute-start = (bf16[384,512]{1,0:T(8,128)(2,1)S(1)}, bf16[384,512]{1,0:T(8,128)(2,1)S(1)}, u32[]{:S(2)}, u32[]{:S(2)}) collective-permute-start(bf16[384,512]{1,0:T(8,128)(2,1)S(1)} %fusion.refs_0_), channel_id=1, source_target_pairs={{0,32},{8,40},{16,48},{24,56},{32,0},{40,8},{48,16},{56,24},{64,96... | collective-permute-start | bytes 1179656 | tf_op jit(solution)/shard_map/ppermute | solution.py:172
  6.5 3.5 %collective-permute-start.2 = (bf16[384,512]{1,0:T(8,128)(2,1)S(1)}, bf16[384,512]{1,0:T(8,128)(2,1)S(1)}, u32[]{:S(2)}, u32[]{:S(2)}) collective-permute-start(bf16[384,512]{1,0:T(8,128)(2,1)S(1)} %fusion.refs_0_), channel_id=1, source_target_pairs={{0,16},{8,24},{16,0},{24,8},{32,48},{40,56},{48,32},{56,40},{64,80... | collective-permute-start | bytes 1179656 | tf_op jit(solution)/shard_map/ppermute | solution.py:172
  10.0 14.2 %collective-permute-done.refs_3_ = bf16[384,512]{1,0:T(8,128)(2,1)S(1)} collective-permute-done((bf16[384,512]{1,0:T(8,128)(2,1)S(1)}, bf16[384,512]{1,0:T(8,128)(2,1)S(1)}, u32[]{:S(2)}, u32[]{:S(2)}) %collective-permute-start) | collective-permute-done | bytes 393248 | tf_op jit(solution)/shard_map/ppermute | solution.py:172
  24.2 2.1 %collective-permute-done.2.refs_1_ = bf16[384,512]{1,0:T(8,128)(2,1)S(1)} collective-permute-done((bf16[384,512]{1,0:T(8,128)(2,1)S(1)}, bf16[384,512]{1,0:T(8,128)(2,1)S(1)}, u32[]{:S(2)}, u32[]{:S(2)}) %collective-permute-start.2) | collective-permute-done | bytes 393248 | tf_op jit(solution)/shard_map/ppermute | solution.py:172
  26.3 2.3 %collective-permute-start.3 = (bf16[384,512]{1,0:T(8,128)(2,1)}, bf16[384,512]{1,0:T(8,128)(2,1)}, u32[]{:S(2)}, u32[]{:S(2)}) collective-permute-start(bf16[384,512]{1,0:T(8,128)(2,1)} %refs_1_.1), channel_id=1, source_target_pairs={{0,32},{8,40},{16,48},{24,56},{32,0},{40,8},{48,16},{56,24},{64,96... | collective-permute-start | bytes 1179656 | tf_op jit(solution)/shard_map/ppermute | solution.py:172
  28.6 2.0 %pad_maximum_fusion = bf16[384,1024]{1,0:T(8,128)(2,1)} fusion(bf16[384,512]{1,0:T(8,128)(2,1)} %refs_1_.1, bf16[384,512]{1,0:T(8,128)(2,1)S(1)} %fusion.refs_0_), kind=kLoop, calls=%fused_computation.2 | loop fusion | flops 1572864 | bytes 1572864 | tf_op jit(solution)/shard_map/concatenate | solution.py:199
  30.6 3.4 %collective-permute-start.7 = (bf16[384,1024]{1,0:T(8,128)(2,1)}, bf16[384,1024]{1,0:T(8,128)(2,1)S(1)}, u32[]{:S(2)}, u32[]{:S(2)}) collective-permute-start(bf16[384,1024]{1,0:T(8,128)(2,1)} %pad_maximum_fusion), channel_id=1, source_target_pairs={{0,1},{1,2},{2,3},{3,4},{4,5},{5,6},{6,7},{8,9},{9,10},{10,11},{11... | collective-permute-start | bytes 2359304 | tf_op jit(solution)/shard_map/ppermute | solution.py:200
  34.0 1.9 %collective-permute-start.10 = (bf16[384,1024]{1,0:T(8,128)(2,1)}, bf16[384,1024]{1,0:T(8,128)(2,1)S(1)}, u32[]{:S(2)}, u32[]{:S(2)}) collective-permute-start(bf16[384,1024]{1,0:T(8,128)(2,1)} %pad_maximum_fusion), channel_id=1, source_target_pairs={{0,8},{8,0},{16,24},{24,16},{32,40},{40,32},{48,56},{56,48},{64,72... | collective-permute-start | bytes 2359304 | tf_op jit(solution)/shard_map/ppermute | solution.py:172
  35.9 7.0 %collective-permute-start.4 = (bf16[384,512]{1,0:T(8,128)(2,1)S(1)}, bf16[384,512]{1,0:T(8,128)(2,1)S(1)}, u32[]{:S(2)}, u32[]{:S(2)}) collective-permute-start(bf16[384,512]{1,0:T(8,128)(2,1)S(1)} %collective-permute-done.refs_3_), channel_id=1, source_target_pairs={{0,96},{8,104},{16,112},{24,120},{32,64},{40,72},{48,80},{56,88},{... | collective-permute-start | bytes 1179656 | tf_op jit(solution)/shard_map/ppermute | solution.py:172
  42.9 8.5 %collective-permute-start.8 = (bf16[384,1024]{1,0:T(8,128)(2,1)}, bf16[384,1024]{1,0:T(8,128)(2,1)S(1)}, u32[]{:S(2)}, u32[]{:S(2)}) collective-permute-start(bf16[384,1024]{1,0:T(8,128)(2,1)} %pad_maximum_fusion), channel_id=1, source_target_pairs={{1,0},{2,1},{3,2},{4,3},{5,4},{6,5},{7,6},{9,8},{10,9},{11,10},{12... | collective-permute-start | bytes 2359304 | tf_op jit(solution)/shard_map/ppermute | solution.py:201
  51.3 0.0 collective-permute-done.3.refs_4_
  51.4 3.4 %collective-permute-start.9 = (bf16[384,1024]{1,0:T(8,128)(2,1)}, bf16[384,1024]{1,0:T(8,128)(2,1)S(1)}, u32[]{:S(2)}, u32[]{:S(2)}) collective-permute-start(bf16[384,1024]{1,0:T(8,128)(2,1)} %pad_maximum_fusion), channel_id=1, source_target_pairs={{0,128},{8,136},{16,144},{24,152},{32,160},{40,168},{48,176},{56,1... | collective-permute-start | bytes 2359304 | tf_op jit(solution)/shard_map/ppermute | solution.py:172
  54.7 5.5 %collective-permute-done.4.refs_3_ = bf16[384,512]{1,0:T(8,128)(2,1)S(1)} collective-permute-done((bf16[384,512]{1,0:T(8,128)(2,1)S(1)}, bf16[384,512]{1,0:T(8,128)(2,1)S(1)}, u32[]{:S(2)}, u32[]{:S(2)}) %collective-permute-start.4) | collective-permute-done | bytes 393248 | tf_op jit(solution)/shard_map/ppermute | solution.py:172
  60.2 0.7 copy-done.3
  61.0 4.3 %collective-permute-start.1 = (bf16[384,1024]{1,0:T(8,128)(2,1)}, bf16[384,1024]{1,0:T(8,128)(2,1)}, u32[]{:S(2)}, u32[]{:S(2)}) collective-permute-start(bf16[384,1024]{1,0:T(8,128)(2,1)} %pad_maximum_fusion), channel_id=1, source_target_pairs={{0,256},{8,264},{16,272},{24,280},{32,288},{40,296},{48,304},{56,3... | collective-permute-start | bytes 2359304 | tf_op jit(solution)/shard_map/ppermute | solution.py:172
  65.3 0.0 collective-permute-done.7.refs_0_
  65.3 4.0 %collective-permute-start.5 = (bf16[384,512]{1,0:T(8,128)(2,1)}, bf16[384,512]{1,0:T(8,128)(2,1)}, u32[]{:S(2)}, u32[]{:S(2)}) collective-permute-start(bf16[384,512]{1,0:T(8,128)(2,1)} %refs_1_.1), channel_id=1, source_target_pairs={{0,16},{8,24},{16,0},{24,8},{32,48},{40,56},{48,32},{56,40},{64,80... | collective-permute-start | bytes 1179656 | tf_op jit(solution)/shard_map/ppermute | solution.py:172
  69.3 0.9 copy-done.5
  70.2 4.4 %collective-permute-start.6 = (bf16[384,512]{1,0:T(8,128)(2,1)}, bf16[384,512]{1,0:T(8,128)(2,1)}, u32[]{:S(2)}, u32[]{:S(2)}) collective-permute-start(bf16[384,512]{1,0:T(8,128)(2,1)} %collective-permute-done.3.refs_4_), channel_id=1, source_target_pairs={{0,96},{8,104},{16,112},{24,120},{32,64},{40,72},{48,80},{56,88},{... | collective-permute-start | bytes 1179656 | tf_op jit(solution)/shard_map/ppermute | solution.py:172
  74.6 0.8 copy.7
  75.4 0.1 reshape.10
  75.5 0.1 pad_add_fusion.scal
  75.6 1.1 copy-done.6
  76.7 3.5 %attend_own_0.1 = (f32[384,512]{1,0:T(8,128)S(1)}, f32[384,512]{1,0:T(8,128)S(1)}, f32[384,512]{1,0:T(8,128)S(1)}) custom-call(s32[57]{0:T(128)S(1)} %pad_add_fusion.scal, bf16[384,512]{1,0:T(8,128)(2,1)S(1)} %copy-done, bf16[384,512]{1,0:T(8,128)(2,1)S(1)} %fusion.refs_0_, bf16[384,512]{1,0:T(8,128)(2,1)} %refs_1_.1, bf16[384,1024]{1,0:T(8,128)(2,1)S(1)} %copy-done.6), custom_call_target="tpu_custom_call" | custom-call | flops 603979776 | bytes 1966080 | tf_op jit(solution)/shard_map/attend_own_0/pallas_call | solution.py:147
  80.2 0.0 collective-permute-done.8.refs_1_
  80.2 41.0 %collective-permute-done.9.refs_2_ = bf16[384,1024]{1,0:T(8,128)(2,1)S(1)} collective-permute-done((bf16[384,1024]{1,0:T(8,128)(2,1)}, bf16[384,1024]{1,0:T(8,128)(2,1)S(1)}, u32[]{:S(2)}, u32[]{:S(2)}) %collective-permute-start.9) | collective-permute-done | bytes 786464 | tf_op jit(solution)/shard_map/ppermute | solution.py:172
  121.2 5.6 %attend_low_high_4_2.1 = (f32[384,512]{1,0:T(8,128)S(1)}, f32[384,512]{1,0:T(8,128)S(1)}, f32[384,512]{1,0:T(8,128)S(1)}) custom-call(s32[57]{0:T(128)S(1)} %pad_add_fusion.scal, bf16[384,512]{1,0:T(8,128)(2,1)S(1)} %copy-done, bf16[384,1024]{1,0:T(8,128)(2,1)S(1)} %collective-permute-done.7.refs_0_, bf16[384,1024]{1,0:T(8,128)(2,1)S(1)} %collective-permute-done.8.refs_1_, ...), custom_call_target="tpu_custom_call" | custom-call | flops 1207959552 | bytes 3932160 | tf_op jit(solution)/shard_map/attend_low_high_4_2/pallas_call | solution.py:147
  126.8 0.0 collective-permute-done.5.refs_2_
  126.8 0.0 collective-permute-done.6.refs_4_
  126.8 5.4 %attend_5_1_3.1 = bf16[384,512]{1,0:T(8,128)(2,1)} custom-call(s32[57]{0:T(128)S(1)} %pad_add_fusion.scal, bf16[384,512]{1,0:T(8,128)(2,1)S(1)} %copy-done, bf16[384,1024]{1,0:T(8,128)(2,1)} %collective-permute-done.1.refs_0_, bf16[384,512]{1,0:T(8,128)(2,1)S(1)} %collective-permute-done.2.refs_1_, bf16[384,512]{1,0:T(8,128)(2,1)} %collective-permute-done.5.refs_2_, ...), custom_call_target="tpu_custom_call" | custom-call | flops 905969664 | bytes 3932160 | tf_op jit(solution)/shard_map/attend_5_1_3/pallas_call | solution.py:147
  (15 shorter events, 0.0 us)
Async XLA Ops:
  1.8 73.7 %copy-start = (bf16[384,512]{1,0:T(8,128)(2,1)S(1)}, bf16[384,512]{1,0:T(8,128)(2,1)}, u32[]{:S(2)}) copy-start(bf16[384,512]{1,0:T(8,128)(2,1)} %q_ref.5) | copy-start | bytes 1179652
  1.8 22.3 %collective-permute-start = (bf16[384,512]{1,0:T(8,128)(2,1)S(1)}, bf16[384,512]{1,0:T(8,128)(2,1)S(1)}, u32[]{:S(2)}, u32[]{:S(2)}) collective-permute-start(bf16[384,512]{1,0:T(8,128)(2,1)S(1)} %fusion.refs_0_), channel_id=1, source_target_pairs={{0,32},{8,40},{16,48},{24,56},{32,0},{40,8},{48,16},{56,24},{64,96... | collective-permute-start | bytes 1179656 | tf_op jit(solution)/shard_map/ppermute | solution.py:172
  6.5 19.8 %collective-permute-start.2 = (bf16[384,512]{1,0:T(8,128)(2,1)S(1)}, bf16[384,512]{1,0:T(8,128)(2,1)S(1)}, u32[]{:S(2)}, u32[]{:S(2)}) collective-permute-start(bf16[384,512]{1,0:T(8,128)(2,1)S(1)} %fusion.refs_0_), channel_id=1, source_target_pairs={{0,16},{8,24},{16,0},{24,8},{32,48},{40,56},{48,32},{56,40},{64,80... | collective-permute-start | bytes 1179656 | tf_op jit(solution)/shard_map/ppermute | solution.py:172
  24.2 11.8 %copy-start.1 = (bf16[384,512]{1,0:T(8,128)(2,1)}, bf16[384,512]{1,0:T(8,128)(2,1)S(1)}, u32[]{:S(2)}) copy-start(bf16[384,512]{1,0:T(8,128)(2,1)S(1)} %collective-permute-done.refs_3_) | copy-start | bytes 1179652
  26.3 25.1 %collective-permute-start.3 = (bf16[384,512]{1,0:T(8,128)(2,1)}, bf16[384,512]{1,0:T(8,128)(2,1)}, u32[]{:S(2)}, u32[]{:S(2)}) collective-permute-start(bf16[384,512]{1,0:T(8,128)(2,1)} %refs_1_.1), channel_id=1, source_target_pairs={{0,32},{8,40},{16,48},{24,56},{32,0},{40,8},{48,16},{56,24},{64,96... | collective-permute-start | bytes 1179656 | tf_op jit(solution)/shard_map/ppermute | solution.py:172
  30.6 34.7 %collective-permute-start.7 = (bf16[384,1024]{1,0:T(8,128)(2,1)}, bf16[384,1024]{1,0:T(8,128)(2,1)S(1)}, u32[]{:S(2)}, u32[]{:S(2)}) collective-permute-start(bf16[384,1024]{1,0:T(8,128)(2,1)} %pad_maximum_fusion), channel_id=1, source_target_pairs={{0,1},{1,2},{2,3},{3,4},{4,5},{5,6},{6,7},{8,9},{9,10},{10,11},{11... | collective-permute-start | bytes 2359304 | tf_op jit(solution)/shard_map/ppermute | solution.py:200
  34.0 35.3 %collective-permute-start.10 = (bf16[384,1024]{1,0:T(8,128)(2,1)}, bf16[384,1024]{1,0:T(8,128)(2,1)S(1)}, u32[]{:S(2)}, u32[]{:S(2)}) collective-permute-start(bf16[384,1024]{1,0:T(8,128)(2,1)} %pad_maximum_fusion), channel_id=1, source_target_pairs={{0,8},{8,0},{16,24},{24,16},{32,40},{40,32},{48,56},{56,48},{64,72... | collective-permute-start | bytes 2359304 | tf_op jit(solution)/shard_map/ppermute | solution.py:172
  35.9 24.3 %collective-permute-start.4 = (bf16[384,512]{1,0:T(8,128)(2,1)S(1)}, bf16[384,512]{1,0:T(8,128)(2,1)S(1)}, u32[]{:S(2)}, u32[]{:S(2)}) collective-permute-start(bf16[384,512]{1,0:T(8,128)(2,1)S(1)} %collective-permute-done.refs_3_), channel_id=1, source_target_pairs={{0,96},{8,104},{16,112},{24,120},{32,64},{40,72},{48,80},{56,88},{... | collective-permute-start | bytes 1179656 | tf_op jit(solution)/shard_map/ppermute | solution.py:172
  42.9 37.3 %collective-permute-start.8 = (bf16[384,1024]{1,0:T(8,128)(2,1)}, bf16[384,1024]{1,0:T(8,128)(2,1)S(1)}, u32[]{:S(2)}, u32[]{:S(2)}) collective-permute-start(bf16[384,1024]{1,0:T(8,128)(2,1)} %pad_maximum_fusion), channel_id=1, source_target_pairs={{1,0},{2,1},{3,2},{4,3},{5,4},{6,5},{7,6},{9,8},{10,9},{11,10},{12... | collective-permute-start | bytes 2359304 | tf_op jit(solution)/shard_map/ppermute | solution.py:201
  51.4 69.8 %collective-permute-start.9 = (bf16[384,1024]{1,0:T(8,128)(2,1)}, bf16[384,1024]{1,0:T(8,128)(2,1)S(1)}, u32[]{:S(2)}, u32[]{:S(2)}) collective-permute-start(bf16[384,1024]{1,0:T(8,128)(2,1)} %pad_maximum_fusion), channel_id=1, source_target_pairs={{0,128},{8,136},{16,144},{24,152},{32,160},{40,168},{48,176},{56,1... | collective-permute-start | bytes 2359304 | tf_op jit(solution)/shard_map/ppermute | solution.py:172
  60.2 0.7 copy-start.3
  61.0 65.8 %collective-permute-start.1 = (bf16[384,1024]{1,0:T(8,128)(2,1)}, bf16[384,1024]{1,0:T(8,128)(2,1)}, u32[]{:S(2)}, u32[]{:S(2)}) collective-permute-start(bf16[384,1024]{1,0:T(8,128)(2,1)} %pad_maximum_fusion), channel_id=1, source_target_pairs={{0,256},{8,264},{16,272},{24,280},{32,288},{40,296},{48,304},{56,3... | collective-permute-start | bytes 2359304 | tf_op jit(solution)/shard_map/ppermute | solution.py:172
  65.3 61.5 %collective-permute-start.5 = (bf16[384,512]{1,0:T(8,128)(2,1)}, bf16[384,512]{1,0:T(8,128)(2,1)}, u32[]{:S(2)}, u32[]{:S(2)}) collective-permute-start(bf16[384,512]{1,0:T(8,128)(2,1)} %refs_1_.1), channel_id=1, source_target_pairs={{0,16},{8,24},{16,0},{24,8},{32,48},{40,56},{48,32},{56,40},{64,80... | collective-permute-start | bytes 1179656 | tf_op jit(solution)/shard_map/ppermute | solution.py:172
  69.3 0.9 copy-start.5
  70.2 56.6 %collective-permute-start.6 = (bf16[384,512]{1,0:T(8,128)(2,1)}, bf16[384,512]{1,0:T(8,128)(2,1)}, u32[]{:S(2)}, u32[]{:S(2)}) collective-permute-start(bf16[384,512]{1,0:T(8,128)(2,1)} %collective-permute-done.3.refs_4_), channel_id=1, source_target_pairs={{0,96},{8,104},{16,112},{24,120},{32,64},{40,72},{48,80},{56,88},{... | collective-permute-start | bytes 1179656 | tf_op jit(solution)/shard_map/ppermute | solution.py:172
  75.6 1.1 copy-start.6
  76.7 44.5 %copy-start.2 = (bf16[384,512]{1,0:T(8,128)(2,1)S(1)}, bf16[384,512]{1,0:T(8,128)(2,1)}, u32[]{:S(2)}) copy-start(bf16[384,512]{1,0:T(8,128)(2,1)} %copy-done.1) | copy-start | bytes 1179652
  121.2 5.6 %copy-start.4 = (bf16[384,512]{1,0:T(8,128)(2,1)S(1)}, bf16[384,512]{1,0:T(8,128)(2,1)}, u32[]{:S(2)}) copy-start(bf16[384,512]{1,0:T(8,128)(2,1)} %copy-done.3) | copy-start | bytes 1179652

commit v2 on v1

--- a/solution.py
+++ b/solution.py
@@ -194,30 +194,20 @@
 
     up = [(i, i + 1) for i in range(space_size - 1)]
     down = [(i + 1, i) for i in range(space_size - 1)]
-    y2_k = partner(marked, 4)
-    y1_k = partner(marked, 2)
     both = jnp.concatenate([marked, values], axis=1)
-    low = lax.ppermute(both, "space", up)
-    high = lax.ppermute(both, "space", down)
+    y4 = partner(both, 8)
+    y2 = partner(both, 4)
+    y1 = partner(both, 2)
+    z2 = partner(both, 32)
     z1 = partner(both, 16)
-    y4_k = partner(y2_k, 12)
-    y2_v = partner(after(values, y2_k, y1_k), 4)
-    z2 = partner(after(both, y2_k), 32)
-    y4_v = partner(after(y2_v, y4_k), 12)
-    y1_v = partner(after(values, y2_v, y4_k), 2)
-    core = partner(after(both, y2_k), 1)
-
-    state = attend(scal, queries, [("own", marked, values), (0, core)], None, False)
-    state = attend(
-        scal,
-        queries,
-        [("low", low), ("high", high), (4, z1), (2, y2_k, y2_v)],
-        state,
-        False,
-    )
-    return attend(
-        scal, queries, [(5, z2), (1, y1_k, y1_v), (3, y4_k, y4_v)], state, True
-    )
+    state = attend(scal, queries, [("own", both)], None, False)
+    second = after(both, z1, z2, state[0])
+    low = lax.ppermute(second, "space", up)
+    high = lax.ppermute(second, "space", down)
+    state = attend(scal, queries, [(4, z1), (5, z2)], state, False)
+    core = partner(after(both, state[0]), 1)
+    state = attend(scal, queries, [(3, y4), (2, y2), (1, y1)], state, False)
+    return attend(scal, queries, [("low", low), ("high", high), (0, core)], state, True)
 
 
 def solution(mesh):

time: 133 us -> 99.4 us (0.75)
  the two profiles are of different devices: /device:TPU:256 before, /device:TPU:392 now
where the time goes in v2:
time: 99.4 us; the launch traced here: 99 us
  waiting for transfers between devices  54.6 us (55%)
  starting transfers between devices  26.6 us (27%)
  Pallas kernels  14.7 us (15%)
  other arithmetic  1.34 us (1%)
    ppermute x6, waiting for transfers between devices, partner(): return lax.ppermute(value, 'tm', [(i, i ^ mask) for i in range(tm_size)])  46.4 us
    ppermute x6, starting transfers between devices, partner(): return lax.ppermute(value, 'tm', [(i, i ^ mask) for i in range(tm_size)])  20.5 us
    pallas_call x4, Pallas kernels, attend(): pl.pallas_call(functools.partial(attend_kernel, kinds, packed, first, las...  14.7 us
    ppermute x1, waiting for transfers between devices, per_device(): low = lax.ppermute(second, 'space', up)  8.24 us
    ppermute x1, starting transfers between devices, per_device(): high = lax.ppermute(second, 'space', down)  3.48 us
    ppermute x1, starting transfers between devices, per_device(): low = lax.ppermute(second, 'space', up)  2.54 us
  transfers between devices with their start and end apart: 8, of which 4 were waited for; matrix products, arithmetic and copies ran while one was open for 1% of the time, Pallas kernels for 10%

profile of v2, /device:TPU:392, one launch (start us, length us, event | category | flops | bytes accessed | tf_op | source)
XLA Modules:
  0.0 99.0 jit_solution(14681607148587279371)
XLA Ops:
  0.0 0.0 copy-start.1
  0.7 1.1 %fusion = bf16[384,512]{1,0:T(8,128)(2,1)S(1)} fusion(bf16[384,512]{1,0:T(8,128)(2,1)} %param.6, s32[]{:T(128)} %bitcast.5, s32[]{:T(128)} %bitcast.4, s32[512]{0:T(512)S(1)} %get-tuple-element.27, s32[512]{0:T(512)S(1)} %get-tuple-element.28, pred[384]{0:T(512)(128)(4,1)S(1)} %fusion.4, pred[512]{0:T(512)(128)(4,1)S(1)} %fusion.3), kind=kLoop, calls=%fused_computation.4 | loop fusion | flops 1572864 | bytes 791432 | tf_op jit(solution)/shard_map/jit(_where)/select_n | solution.py:193
  1.9 0.0 copy-done.1
  1.9 0.0 copy-start
  1.9 0.1 pad_maximum_fusion.refs_0_
  2.0 2.5 %collective-permute-start.1 = (bf16[384,1024]{1,0:T(8,128)(2,1)S(1)}, bf16[384,1024]{1,0:T(8,128)(2,1)S(1)}, u32[]{:S(2)}, u32[]{:S(2)}) collective-permute-start(bf16[384,1024]{1,0:T(8,128)(2,1)S(1)} %pad_maximum_fusion.refs_0_), channel_id=1, source_target_pairs={{0,256},{8,264},{16,272},{24,280},{32,288},{40,296},{48,304},{56,3... | collective-permute-start | bytes 2359304 | tf_op jit(solution)/shard_map/ppermute | solution.py:172
  4.5 3.4 %collective-permute-start = (bf16[384,1024]{1,0:T(8,128)(2,1)S(1)}, bf16[384,1024]{1,0:T(8,128)(2,1)S(1)}, u32[]{:S(2)}, u32[]{:S(2)}) collective-permute-start(bf16[384,1024]{1,0:T(8,128)(2,1)S(1)} %pad_maximum_fusion.refs_0_), channel_id=1, source_target_pairs={{0,128},{8,136},{16,144},{24,152},{32,160},{40,168},{48,176},{56,1... | collective-permute-start | bytes 2359304 | tf_op jit(solution)/shard_map/ppermute | solution.py:172
  7.9 2.4 %collective-permute-start.7 = (bf16[384,1024]{1,0:T(8,128)(2,1)S(1)}, bf16[384,1024]{1,0:T(8,128)(2,1)S(1)}, u32[]{:S(2)}, u32[]{:S(2)}) collective-permute-start(bf16[384,1024]{1,0:T(8,128)(2,1)S(1)} %pad_maximum_fusion.refs_0_), channel_id=1, source_target_pairs={{0,16},{8,24},{16,0},{24,8},{32,48},{40,56},{48,32},{56,40},{64,80... | collective-permute-start | bytes 2359304 | tf_op jit(solution)/shard_map/ppermute | solution.py:172
  10.2 4.5 %collective-permute-start.6 = (bf16[384,1024]{1,0:T(8,128)(2,1)S(1)}, bf16[384,1024]{1,0:T(8,128)(2,1)}, u32[]{:S(2)}, u32[]{:S(2)}) collective-permute-start(bf16[384,1024]{1,0:T(8,128)(2,1)S(1)} %pad_maximum_fusion.refs_0_), channel_id=1, source_target_pairs={{0,32},{8,40},{16,48},{24,56},{32,0},{40,8},{48,16},{56,24},{64,96... | collective-permute-start | bytes 2359304 | tf_op jit(solution)/shard_map/ppermute | solution.py:172
  14.7 5.9 %collective-permute-start.5 = (bf16[384,1024]{1,0:T(8,128)(2,1)S(1)}, bf16[384,1024]{1,0:T(8,128)(2,1)}, u32[]{:S(2)}, u32[]{:S(2)}) collective-permute-start(bf16[384,1024]{1,0:T(8,128)(2,1)S(1)} %pad_maximum_fusion.refs_0_), channel_id=1, source_target_pairs={{0,64},{8,72},{16,80},{24,88},{32,96},{40,104},{48,112},{56,120},{... | collective-permute-start | bytes 2359304 | tf_op jit(solution)/shard_map/ppermute | solution.py:172
  20.7 0.8 copy.7
  21.5 0.1 reshape.10
  21.6 0.1 pad_add_fusion.scal
  21.6 0.0 copy-done
  21.7 2.0 %attend_own.1 = (f32[384,512]{1,0:T(8,128)S(1)}, f32[384,512]{1,0:T(8,128)S(1)}, f32[384,512]{1,0:T(8,128)S(1)}) custom-call(s32[57]{0:T(128)S(1)} %pad_add_fusion.scal, bf16[384,512]{1,0:T(8,128)(2,1)S(1)} %copy-done, bf16[384,1024]{1,0:T(8,128)(2,1)S(1)} %pad_maximum_fusion.refs_0_), custom_call_target="tpu_custom_call" | custom-call | flops 301989888 | bytes 1179648 | tf_op jit(solution)/shard_map/attend_own/pallas_call | solution.py:147
  23.7 14.5 %collective-permute-done.1.refs_1_ = bf16[384,1024]{1,0:T(8,128)(2,1)S(1)} collective-permute-done((bf16[384,1024]{1,0:T(8,128)(2,1)S(1)}, bf16[384,1024]{1,0:T(8,128)(2,1)S(1)}, u32[]{:S(2)}, u32[]{:S(2)}) %collective-permute-start.1) | collective-permute-done | bytes 786464 | tf_op jit(solution)/shard_map/ppermute | solution.py:172
  38.1 3.0 %collective-permute-done.refs_0_ = bf16[384,1024]{1,0:T(8,128)(2,1)S(1)} collective-permute-done((bf16[384,1024]{1,0:T(8,128)(2,1)S(1)}, bf16[384,1024]{1,0:T(8,128)(2,1)S(1)}, u32[]{:S(2)}, u32[]{:S(2)}) %collective-permute-start) | collective-permute-done | bytes 786464 | tf_op jit(solution)/shard_map/ppermute | solution.py:172
  41.1 3.3 %attend_4_5.1 = (f32[384,512]{1,0:T(8,128)S(1)}, f32[384,512]{1,0:T(8,128)S(1)}, f32[384,512]{1,0:T(8,128)S(1)}) custom-call(s32[57]{0:T(128)S(1)} %pad_add_fusion.scal, bf16[384,512]{1,0:T(8,128)(2,1)S(1)} %copy-done, bf16[384,1024]{1,0:T(8,128)(2,1)S(1)} %collective-permute-done.refs_0_, bf16[384,1024]{1,0:T(8,128)(2,1)S(1)} %collective-permute-done.1.refs_1_, ...), custom_call_target="tpu_custom_call" | custom-call | flops 603979776 | bytes 2752512 | tf_op jit(solution)/shard_map/attend_4_5/pallas_call | solution.py:147
  44.4 1.9 %collective-permute-start.4 = (bf16[384,1024]{1,0:T(8,128)(2,1)S(1)}, bf16[384,1024]{1,0:T(8,128)(2,1)S(1)}, u32[]{:S(2)}, u32[]{:S(2)}) collective-permute-start(bf16[384,1024]{1,0:T(8,128)(2,1)S(1)} %pad_maximum_fusion.refs_0_), channel_id=1, source_target_pairs={{0,8},{8,0},{16,24},{24,16},{32,40},{40,32},{48,56},{56,48},{64,72... | collective-permute-start | bytes 2359304 | tf_op jit(solution)/shard_map/ppermute | solution.py:172
  46.3 3.5 %collective-permute-start.3 = (bf16[384,1024]{1,0:T(8,128)(2,1)S(1)}, bf16[384,1024]{1,0:T(8,128)(2,1)S(1)}, u32[]{:S(2)}, u32[]{:S(2)}) collective-permute-start(bf16[384,1024]{1,0:T(8,128)(2,1)S(1)} %pad_maximum_fusion.refs_0_), channel_id=1, source_target_pairs={{1,0},{2,1},{3,2},{4,3},{5,4},{6,5},{7,6},{9,8},{10,9},{11,10},{12... | collective-permute-start | bytes 2359304 | tf_op jit(solution)/shard_map/ppermute | solution.py:206
  49.8 0.0 collective-permute-done.7.refs_2_
  49.8 2.5 %collective-permute-start.2 = (bf16[384,1024]{1,0:T(8,128)(2,1)S(1)}, bf16[384,1024]{1,0:T(8,128)(2,1)S(1)}, u32[]{:S(2)}, u32[]{:S(2)}) collective-permute-start(bf16[384,1024]{1,0:T(8,128)(2,1)S(1)} %pad_maximum_fusion.refs_0_), channel_id=1, source_target_pairs={{0,1},{1,2},{2,3},{3,4},{4,5},{5,6},{6,7},{8,9},{9,10},{10,11},{11... | collective-permute-start | bytes 2359304 | tf_op jit(solution)/shard_map/ppermute | solution.py:205
  52.4 28.9 %collective-permute-done.6.refs_1_ = bf16[384,1024]{1,0:T(8,128)(2,1)} collective-permute-done((bf16[384,1024]{1,0:T(8,128)(2,1)S(1)}, bf16[384,1024]{1,0:T(8,128)(2,1)}, u32[]{:S(2)}, u32[]{:S(2)}) %collective-permute-start.6) | collective-permute-done | bytes 786464 | tf_op jit(solution)/shard_map/ppermute | solution.py:172
  81.3 0.0 collective-permute-done.5.refs_0_
  81.3 4.7 %attend_3_2_1.1 = (f32[384,512]{1,0:T(8,128)S(1)}, f32[384,512]{1,0:T(8,128)S(1)}, f32[384,512]{1,0:T(8,128)S(1)}) custom-call(s32[57]{0:T(128)S(1)} %pad_add_fusion.scal, bf16[384,512]{1,0:T(8,128)(2,1)S(1)} %copy-done, bf16[384,1024]{1,0:T(8,128)(2,1)} %collective-permute-done.5.refs_0_, bf16[384,1024]{1,0:T(8,128)(2,1)} %collective-permute-done.6.refs_1_, ...), custom_call_target="tpu_custom_call" | custom-call | flops 905969664 | bytes 3145728 | tf_op jit(solution)/shard_map/attend_3_2_1/pallas_call | solution.py:147
  86.0 0.0 collective-permute-done.4.refs_2_
  86.0 0.0 collective-permute-done.3.refs_1_
  86.0 8.2 %collective-permute-done.2.refs_0_ = bf16[384,1024]{1,0:T(8,128)(2,1)S(1)} collective-permute-done((bf16[384,1024]{1,0:T(8,128)(2,1)S(1)}, bf16[384,1024]{1,0:T(8,128)(2,1)S(1)}, u32[]{:S(2)}, u32[]{:S(2)}) %collective-permute-start.2) | collective-permute-done | bytes 786464 | tf_op jit(solution)/shard_map/ppermute | solution.py:205
  94.2 4.8 %attend_low_high_0.1 = bf16[384,512]{1,0:T(8,128)(2,1)} custom-call(s32[57]{0:T(128)S(1)} %pad_add_fusion.scal, bf16[384,512]{1,0:T(8,128)(2,1)S(1)} %copy-done, bf16[384,1024]{1,0:T(8,128)(2,1)S(1)} %collective-permute-done.2.refs_0_, bf16[384,1024]{1,0:T(8,128)(2,1)S(1)} %collective-permute-done.3.refs_1_, ...), custom_call_target="tpu_custom_call" | custom-call | flops 905969664 | bytes 3145728 | tf_op jit(solution)/shard_map/attend_low_high_0/pallas_call | solution.py:147
  (3 shorter events, 0.0 us)
Async XLA Ops:
  0.0 1.9 %copy-start.1 = (bf16[384,512]{1,0:T(8,128)(2,1)S(1)}, bf16[384,512]{1,0:T(8,128)(2,1)}, u32[]{:S(2)}) copy-start(bf16[384,512]{1,0:T(8,128)(2,1)} %param.7) | copy-start | bytes 1179652
  1.9 19.8 %copy-start = (bf16[384,512]{1,0:T(8,128)(2,1)S(1)}, bf16[384,512]{1,0:T(8,128)(2,1)}, u32[]{:S(2)}) copy-start(bf16[384,512]{1,0:T(8,128)(2,1)} %q_ref.7) | copy-start | bytes 1179652
  2.0 36.1 %collective-permute-start.1 = (bf16[384,1024]{1,0:T(8,128)(2,1)S(1)}, bf16[384,1024]{1,0:T(8,128)(2,1)S(1)}, u32[]{:S(2)}, u32[]{:S(2)}) collective-permute-start(bf16[384,1024]{1,0:T(8,128)(2,1)S(1)} %pad_maximum_fusion.refs_0_), channel_id=1, source_target_pairs={{0,256},{8,264},{16,272},{24,280},{32,288},{40,296},{48,304},{56,3... | collective-permute-start | bytes 2359304 | tf_op jit(solution)/shard_map/ppermute | solution.py:172
  4.5 36.6 %collective-permute-start = (bf16[384,1024]{1,0:T(8,128)(2,1)S(1)}, bf16[384,1024]{1,0:T(8,128)(2,1)S(1)}, u32[]{:S(2)}, u32[]{:S(2)}) collective-permute-start(bf16[384,1024]{1,0:T(8,128)(2,1)S(1)} %pad_maximum_fusion.refs_0_), channel_id=1, source_target_pairs={{0,128},{8,136},{16,144},{24,152},{32,160},{40,168},{48,176},{56,1... | collective-permute-start | bytes 2359304 | tf_op jit(solution)/shard_map/ppermute | solution.py:172
  7.9 41.9 %collective-permute-start.7 = (bf16[384,1024]{1,0:T(8,128)(2,1)S(1)}, bf16[384,1024]{1,0:T(8,128)(2,1)S(1)}, u32[]{:S(2)}, u32[]{:S(2)}) collective-permute-start(bf16[384,1024]{1,0:T(8,128)(2,1)S(1)} %pad_maximum_fusion.refs_0_), channel_id=1, source_target_pairs={{0,16},{8,24},{16,0},{24,8},{32,48},{40,56},{48,32},{56,40},{64,80... | collective-permute-start | bytes 2359304 | tf_op jit(solution)/shard_map/ppermute | solution.py:172
  10.2 71.1 %collective-permute-start.6 = (bf16[384,1024]{1,0:T(8,128)(2,1)S(1)}, bf16[384,1024]{1,0:T(8,128)(2,1)}, u32[]{:S(2)}, u32[]{:S(2)}) collective-permute-start(bf16[384,1024]{1,0:T(8,128)(2,1)S(1)} %pad_maximum_fusion.refs_0_), channel_id=1, source_target_pairs={{0,32},{8,40},{16,48},{24,56},{32,0},{40,8},{48,16},{56,24},{64,96... | collective-permute-start | bytes 2359304 | tf_op jit(solution)/shard_map/ppermute | solution.py:172
  14.7 66.5 %collective-permute-start.5 = (bf16[384,1024]{1,0:T(8,128)(2,1)S(1)}, bf16[384,1024]{1,0:T(8,128)(2,1)}, u32[]{:S(2)}, u32[]{:S(2)}) collective-permute-start(bf16[384,1024]{1,0:T(8,128)(2,1)S(1)} %pad_maximum_fusion.refs_0_), channel_id=1, source_target_pairs={{0,64},{8,72},{16,80},{24,88},{32,96},{40,104},{48,112},{56,120},{... | collective-permute-start | bytes 2359304 | tf_op jit(solution)/shard_map/ppermute | solution.py:172
  44.4 41.6 %collective-permute-start.4 = (bf16[384,1024]{1,0:T(8,128)(2,1)S(1)}, bf16[384,1024]{1,0:T(8,128)(2,1)S(1)}, u32[]{:S(2)}, u32[]{:S(2)}) collective-permute-start(bf16[384,1024]{1,0:T(8,128)(2,1)S(1)} %pad_maximum_fusion.refs_0_), channel_id=1, source_target_pairs={{0,8},{8,0},{16,24},{24,16},{32,40},{40,32},{48,56},{56,48},{64,72... | collective-permute-start | bytes 2359304 | tf_op jit(solution)/shard_map/ppermute | solution.py:172
  46.3 39.7 %collective-permute-start.3 = (bf16[384,1024]{1,0:T(8,128)(2,1)S(1)}, bf16[384,1024]{1,0:T(8,128)(2,1)S(1)}, u32[]{:S(2)}, u32[]{:S(2)}) collective-permute-start(bf16[384,1024]{1,0:T(8,128)(2,1)S(1)} %pad_maximum_fusion.refs_0_), channel_id=1, source_target_pairs={{1,0},{2,1},{3,2},{4,3},{5,4},{6,5},{7,6},{9,8},{10,9},{11,10},{12... | collective-permute-start | bytes 2359304 | tf_op jit(solution)/shard_map/ppermute | solution.py:206
  49.8 44.4 %collective-permute-start.2 = (bf16[384,1024]{1,0:T(8,128)(2,1)S(1)}, bf16[384,1024]{1,0:T(8,128)(2,1)S(1)}, u32[]{:S(2)}, u32[]{:S(2)}) collective-permute-start(bf16[384,1024]{1,0:T(8,128)(2,1)S(1)} %pad_maximum_fusion.refs_0_), channel_id=1, source_target_pairs={{0,1},{1,2},{2,3},{3,4},{4,5},{5,6},{6,7},{8,9},{9,10},{10,11},{11... | collective-permute-start | bytes 2359304 | tf_op jit(solution)/shard_map/ppermute | solution.py:205

commit v3 on v2

--- a/solution.py
+++ b/solution.py
@@ -69,22 +69,25 @@
                 break
         valid.append(per_q)
 
-    for h in range(heads):
+    def head_scores(h):
         hs = slice(h * HEAD, (h + 1) * HEAD)
-        q = q_ref[:, hs]
-        scores = []
+        keys = jnp.concatenate([k_ref[:, hs] for k_ref, _, _ in tiles], axis=0)
+        return lax.dot_general(
+            q_ref[:, hs], keys, (((1,), (1,)), ((), ())), preferred_element_type=jnp.float32
+        )
+
+    def head_finish(h, s):
+        hs = slice(h * HEAD, (h + 1) * HEAD)
         top = None
-        for t, (k_ref, _, _) in enumerate(tiles):
-            s = lax.dot_general(
-                q, k_ref[:, hs], (((1,), (1,)), ((), ())), preferred_element_type=jnp.float32
-            )
-            cols = []
+        cols = []
+        for t in range(len(tiles)):
             for kb in range(blocks):
+                at = (t * blocks + kb) * BLK
                 col = jnp.concatenate(
                     [
                         jnp.where(
                             valid[t][qb][kb],
-                            s[qb * BLK : (qb + 1) * BLK, kb * BLK : (kb + 1) * BLK],
+                            s[qb * BLK : (qb + 1) * BLK, at : at + BLK],
                             jnp.float32(NEG),
                         )
                         for qb in range(blocks)
@@ -93,38 +96,39 @@
                 )
                 cols.append(col)
                 top = col if top is None else jnp.maximum(top, col)
-            scores.append(cols)
         top = jnp.broadcast_to(jnp.max(top, axis=1, keepdims=True), (rows, HEAD))
         if not first:
             m_old = m_in[:, hs]
             top = jnp.maximum(top, m_old)
         top_s = top * scale
-        total = None
-        acc = None
+        probs = [jnp.exp2(col * scale - top_s).astype(jnp.bfloat16) for col in cols]
+        vals = []
+        for _, v_ref, v_off in tiles:
+            v = v_ref[:, v_off + h * HEAD : v_off + (h + 1) * HEAD]
+            vals.append(jnp.concatenate([v, jnp.ones_like(v)], axis=1))
+        part = jnp.dot(
+            jnp.concatenate(probs, axis=1),
+            jnp.concatenate(vals, axis=0),
+            preferred_element_type=jnp.float32,
+        )
+        acc, total = part[:, :HEAD], part[:, HEAD:]
         if not first:
             alpha = jnp.exp2(m_old * scale - top_s)
-            total = l_in[:, hs] * alpha
-            acc = a_in[:, hs] * alpha
-        for t, (_, v_ref, v_off) in enumerate(tiles):
-            probs = []
-            for kb in range(blocks):
-                p = jnp.exp2(scores[t][kb] * scale - top_s)
-                total = p if total is None else total + p
-                probs.append(p.astype(jnp.bfloat16))
-            part = jnp.dot(
-                jnp.concatenate(probs, axis=1),
-                v_ref[:, v_off + h * HEAD : v_off + (h + 1) * HEAD],
-                preferred_element_type=jnp.float32,
-            )
-            acc = part if acc is None else acc + part
+            total = total + l_in[:, hs] * alpha
+            acc = acc + a_in[:, hs] * alpha
         if last:
-            norm = 1.0 / jnp.sum(total, axis=1, keepdims=True)
             live = lax.broadcasted_iota(jnp.int32, (rows, HEAD), 0) < scal[0]
-            out_ref[:, hs] = jnp.where(live, acc * norm, 0.0).astype(out_ref.dtype)
+            out_ref[:, hs] = jnp.where(live, acc / total, 0.0).astype(out_ref.dtype)
         else:
             m_out[:, hs] = top
             l_out[:, hs] = total
             a_out[:, hs] = acc
+
+    ready = head_scores(0)
+    for h in range(heads):
+        following = head_scores(h + 1) if h + 1 < heads else None
+        head_finish(h, ready)
+        ready = following
 
 
 def attend(scal, q, tiles, state, last):
@@ -195,19 +199,22 @@
     up = [(i, i + 1) for i in range(space_size - 1)]
     down = [(i + 1, i) for i in range(space_size - 1)]
     both = jnp.concatenate([marked, values], axis=1)
-    y4 = partner(both, 8)
-    y2 = partner(both, 4)
+    y2_k = partner(marked, 4)
+    y4_v = partner(values, 8)
     y1 = partner(both, 2)
     z2 = partner(both, 32)
     z1 = partner(both, 16)
-    state = attend(scal, queries, [("own", both)], None, False)
+    core = partner(both, 1)
+    state = attend(scal, queries, [("own", both), (0, core)], None, False)
+    y4_k = partner(after(y2_k, state[0]), 12)
+    y2_v = partner(after(values, y2_k, y4_v, state[0]), 4)
     second = after(both, z1, z2, state[0])
     low = lax.ppermute(second, "space", up)
     high = lax.ppermute(second, "space", down)
     state = attend(scal, queries, [(4, z1), (5, z2)], state, False)
-    core = partner(after(both, state[0]), 1)
-    state = attend(scal, queries, [(3, y4), (2, y2), (1, y1)], state, False)
-    return attend(scal, queries, [("low", low), ("high", high), (0, core)], state, True)
+    state = attend(scal, queries, [(1, y1)], state, False)
+    state = attend(scal, queries, [(3, y4_k, y4_v), (2, y2_k, y2_v)], state, False)
+    return attend(scal, queries, [("low", low), ("high", high)], state, True)
 
 
 def solution(mesh):

time: 99.4 us -> 96.5 us (0.971)
  waiting for transfers between devices: 54.6 us -> 41.7 us
  starting transfers between devices: 26.6 us -> 35.7 us
  other arithmetic: 1.34 us -> 3.24 us
  Pallas kernels: 14.7 us -> 13.7 us
    ppermute x6 -> x8, waiting for transfers between devices: 46.4 us -> 30.7 us  [partner(): return lax.ppermute(value, 'tm', [(i, i ^ mask) for i in range(tm_size)])]
    ppermute x6 -> x8, starting transfers between devices: 20.5 us -> 29.9 us  [partner(): return lax.ppermute(value, 'tm', [(i, i ^ mask) for i in range(tm_size)])]
    ppermute x1, waiting for transfers between devices: 8.24 us -> 10.1 us  [per_device(): low = lax.ppermute(second, 'space', up)]
    concatenate x1, other arithmetic: 0.1 us -> 1.24 us  [per_device(): both = jnp.concatenate([marked, values], axis=1)]
    pallas_call x4 -> x5, Pallas kernels: 14.7 us -> 13.7 us  [attend(): pl.pallas_call(functools.partial(attend_kernel, kinds, packed, first, las...]
  transfers between devices with their start and end apart: 8 -> 10, of which waited for: 4 -> 6; matrix products, arithmetic and copies ran while one was open for 1% -> 1% of each run, Pallas kernels for 10% -> 11%
where the time goes in v3:
time: 96.5 us; the launch traced here: 96 us
  waiting for transfers between devices  41.7 us (43%)
  starting transfers between devices  35.7 us (37%)
  Pallas kernels  13.7 us (14%)
  other arithmetic  3.24 us (3%)
    ppermute x8, waiting for transfers between devices, partner(): return lax.ppermute(value, 'tm', [(i, i ^ mask) for i in range(tm_size)])  30.7 us
    ppermute x8, starting transfers between devices, partner(): return lax.ppermute(value, 'tm', [(i, i ^ mask) for i in range(tm_size)])  29.9 us
    pallas_call x5, Pallas kernels, attend(): pl.pallas_call(functools.partial(attend_kernel, kinds, packed, first, las...  13.7 us
    ppermute x1, waiting for transfers between devices, per_device(): low = lax.ppermute(second, 'space', up)  10.1 us
    ppermute x1, starting transfers between devices, per_device(): high = lax.ppermute(second, 'space', down)  3.46 us
    ppermute x1, starting transfers between devices, per_device(): low = lax.ppermute(second, 'space', up)  2.37 us
  transfers between devices with their start and end apart: 10, of which 6 were waited for; matrix products, arithmetic and copies ran while one was open for 1% of the time, Pallas kernels for 11%

profile of v3, /device:TPU:392, one launch (start us, length us, event | category | flops | bytes accessed | tf_op | source)
XLA Modules:
  0.0 96.0 jit_solution(6841534953939185297)
XLA Ops:
  0.7 1.9 %fusion = bf16[384,512]{1,0:T(8,128)(2,1)} fusion(bf16[384,512]{1,0:T(8,128)(2,1)} %param.6, s32[]{:T(128)} %bitcast.5, s32[]{:T(128)} %bitcast.4, s32[512]{0:T(512)S(1)} %get-tuple-element.35, s32[512]{0:T(512)S(1)} %get-tuple-element.36, pred[384]{0:T(512)(128)(4,1)S(1)} %fusion.4, pred[512]{0:T(512)(128)(4,1)S(1)} %fusion.3), kind=kLoop, calls=%fused_computation.4 | loop fusion | flops 1572864 | bytes 791432 | tf_op jit(solution)/shard_map/jit(_where)/select_n | solution.py:197
  2.6 0.0 copy-start
  2.6 1.2 %pad_maximum_fusion.refs_0_ = bf16[384,1024]{1,0:T(8,128)(2,1)S(1)} fusion(bf16[384,512]{1,0:T(8,128)(2,1)} %param.7, bf16[384,512]{1,0:T(8,128)(2,1)} %fusion), kind=kLoop, calls=%fused_computation.2 | loop fusion | flops 1572864 | bytes 1572864 | tf_op jit(solution)/shard_map/concatenate | solution.py:201
  3.8 1.9 %collective-permute-start.2 = (bf16[384,1024]{1,0:T(8,128)(2,1)S(1)}, bf16[384,1024]{1,0:T(8,128)(2,1)}, u32[]{:S(2)}, u32[]{:S(2)}) collective-permute-start(bf16[384,1024]{1,0:T(8,128)(2,1)S(1)} %pad_maximum_fusion.refs_0_), channel_id=1, source_target_pairs={{0,8},{8,0},{16,24},{24,16},{32,40},{40,32},{48,56},{56,48},{64,72... | collective-permute-start | bytes 2359304 | tf_op jit(solution)/shard_map/ppermute | solution.py:176
  5.8 2.5 %collective-permute-start.1 = (bf16[384,1024]{1,0:T(8,128)(2,1)S(1)}, bf16[384,1024]{1,0:T(8,128)(2,1)S(1)}, u32[]{:S(2)}, u32[]{:S(2)}) collective-permute-start(bf16[384,1024]{1,0:T(8,128)(2,1)S(1)} %pad_maximum_fusion.refs_0_), channel_id=1, source_target_pairs={{0,256},{8,264},{16,272},{24,280},{32,288},{40,296},{48,304},{56,3... | collective-permute-start | bytes 2359304 | tf_op jit(solution)/shard_map/ppermute | solution.py:176
  8.2 3.4 %collective-permute-start = (bf16[384,1024]{1,0:T(8,128)(2,1)S(1)}, bf16[384,1024]{1,0:T(8,128)(2,1)S(1)}, u32[]{:S(2)}, u32[]{:S(2)}) collective-permute-start(bf16[384,1024]{1,0:T(8,128)(2,1)S(1)} %pad_maximum_fusion.refs_0_), channel_id=1, source_target_pairs={{0,128},{8,136},{16,144},{24,152},{32,160},{40,168},{48,176},{56,1... | collective-permute-start | bytes 2359304 | tf_op jit(solution)/shard_map/ppermute | solution.py:176
  11.6 4.5 %collective-permute-start.5 = (bf16[384,512]{1,0:T(8,128)(2,1)}, bf16[384,512]{1,0:T(8,128)(2,1)S(1)}, u32[]{:S(2)}, u32[]{:S(2)}) collective-permute-start(bf16[384,512]{1,0:T(8,128)(2,1)} %fusion), channel_id=1, source_target_pairs={{0,32},{8,40},{16,48},{24,56},{32,0},{40,8},{48,16},{56,24},{64,96... | collective-permute-start | bytes 1179656 | tf_op jit(solution)/shard_map/ppermute | solution.py:176
  16.1 5.0 %collective-permute-start.7 = (bf16[384,512]{1,0:T(8,128)(2,1)}, bf16[384,512]{1,0:T(8,128)(2,1)S(1)}, u32[]{:S(2)}, u32[]{:S(2)}) collective-permute-start(bf16[384,512]{1,0:T(8,128)(2,1)} %param.7), channel_id=1, source_target_pairs={{0,64},{8,72},{16,80},{24,88},{32,96},{40,104},{48,112},{56,120},{... | collective-permute-start | bytes 1179656 | tf_op jit(solution)/shard_map/ppermute | solution.py:176
  21.2 0.8 copy.7
  22.0 0.1 reshape.10
  22.1 0.0 collective-permute-done.2.refs_1_
  22.1 3.3 %collective-permute-start.9 = (bf16[384,1024]{1,0:T(8,128)(2,1)S(1)}, bf16[384,1024]{1,0:T(8,128)(2,1)S(1)}, u32[]{:S(2)}, u32[]{:S(2)}) collective-permute-start(bf16[384,1024]{1,0:T(8,128)(2,1)S(1)} %pad_maximum_fusion.refs_0_), channel_id=1, source_target_pairs={{0,16},{8,24},{16,0},{24,8},{32,48},{40,56},{48,32},{56,40},{64,80... | collective-permute-start | bytes 2359304 | tf_op jit(solution)/shard_map/ppermute | solution.py:176
  25.3 0.1 pad_add_fusion.scal
  25.4 0.0 copy-done
  25.4 3.1 %attend_own_0.1 = (f32[384,512]{1,0:T(8,128)S(1)}, f32[384,512]{1,0:T(8,128)S(1)}, f32[384,512]{1,0:T(8,128)S(1)}) custom-call(s32[57]{0:T(128)S(1)} %pad_add_fusion.scal, bf16[384,512]{1,0:T(8,128)(2,1)S(1)} %copy-done, bf16[384,1024]{1,0:T(8,128)(2,1)S(1)} %pad_maximum_fusion.refs_0_, bf16[384,1024]{1,0:T(8,128)(2,1)} %collective-permute-done.2.refs_1_), custom_call_target="tpu_custom_call" | custom-call | flops 603979776 | bytes 1572864 | tf_op jit(solution)/shard_map/attend_own_0/pallas_call | solution.py:151
  28.5 14.1 %collective-permute-done.1.refs_1_ = bf16[384,1024]{1,0:T(8,128)(2,1)S(1)} collective-permute-done((bf16[384,1024]{1,0:T(8,128)(2,1)S(1)}, bf16[384,1024]{1,0:T(8,128)(2,1)S(1)}, u32[]{:S(2)}, u32[]{:S(2)}) %collective-permute-start.1) | collective-permute-done | bytes 786464 | tf_op jit(solution)/shard_map/ppermute | solution.py:176
  42.6 3.0 %collective-permute-done.refs_0_ = bf16[384,1024]{1,0:T(8,128)(2,1)S(1)} collective-permute-done((bf16[384,1024]{1,0:T(8,128)(2,1)S(1)}, bf16[384,1024]{1,0:T(8,128)(2,1)S(1)}, u32[]{:S(2)}, u32[]{:S(2)}) %collective-permute-start) | collective-permute-done | bytes 786464 | tf_op jit(solution)/shard_map/ppermute | solution.py:176
  45.5 3.5 %collective-permute-start.4 = (bf16[384,1024]{1,0:T(8,128)(2,1)S(1)}, bf16[384,1024]{1,0:T(8,128)(2,1)S(1)}, u32[]{:S(2)}, u32[]{:S(2)}) collective-permute-start(bf16[384,1024]{1,0:T(8,128)(2,1)S(1)} %pad_maximum_fusion.refs_0_), channel_id=1, source_target_pairs={{1,0},{2,1},{3,2},{4,3},{5,4},{6,5},{7,6},{9,8},{10,9},{11,10},{12... | collective-permute-start | bytes 2359304 | tf_op jit(solution)/shard_map/ppermute | solution.py:213
  49.0 2.4 %collective-permute-start.3 = (bf16[384,1024]{1,0:T(8,128)(2,1)S(1)}, bf16[384,1024]{1,0:T(8,128)(2,1)S(1)}, u32[]{:S(2)}, u32[]{:S(2)}) collective-permute-start(bf16[384,1024]{1,0:T(8,128)(2,1)S(1)} %pad_maximum_fusion.refs_0_), channel_id=1, source_target_pairs={{0,1},{1,2},{2,3},{3,4},{4,5},{5,6},{6,7},{8,9},{9,10},{10,11},{11... | collective-permute-start | bytes 2359304 | tf_op jit(solution)/shard_map/ppermute | solution.py:212
  51.4 0.0 collective-permute-done.5.refs_2_
  51.4 0.0 collective-permute-done.7.refs_1_
  51.4 5.3 %collective-permute-start.6 = (bf16[384,512]{1,0:T(8,128)(2,1)S(1)}, bf16[384,512]{1,0:T(8,128)(2,1)S(1)}, u32[]{:S(2)}, u32[]{:S(2)}) collective-permute-start(bf16[384,512]{1,0:T(8,128)(2,1)S(1)} %collective-permute-done.5.refs_2_), channel_id=1, source_target_pairs={{0,96},{8,104},{16,112},{24,120},{32,64},{40,72},{48,80},{56,88},{... | collective-permute-start | bytes 1179656 | tf_op jit(solution)/shard_map/ppermute | solution.py:176
  56.7 4.0 %collective-permute-start.8 = (bf16[384,512]{1,0:T(8,128)(2,1)}, bf16[384,512]{1,0:T(8,128)(2,1)S(1)}, u32[]{:S(2)}, u32[]{:S(2)}) collective-permute-start(bf16[384,512]{1,0:T(8,128)(2,1)} %param.7), channel_id=1, source_target_pairs={{0,32},{8,40},{16,48},{24,56},{32,0},{40,8},{48,16},{56,24},{64,96... | collective-permute-start | bytes 1179656 | tf_op jit(solution)/shard_map/ppermute | solution.py:176
  60.7 2.6 %attend_4_5.1 = (f32[384,512]{1,0:T(8,128)S(1)}, f32[384,512]{1,0:T(8,128)S(1)}, f32[384,512]{1,0:T(8,128)S(1)}) custom-call(s32[57]{0:T(128)S(1)} %pad_add_fusion.scal, bf16[384,512]{1,0:T(8,128)(2,1)S(1)} %copy-done, bf16[384,1024]{1,0:T(8,128)(2,1)S(1)} %collective-permute-done.refs_0_, bf16[384,1024]{1,0:T(8,128)(2,1)S(1)} %collective-permute-done.1.refs_1_, ...), custom_call_target="tpu_custom_call" | custom-call | flops 603979776 | bytes 2752512 | tf_op jit(solution)/shard_map/attend_4_5/pallas_call | solution.py:151
  63.4 7.1 %collective-permute-done.9.refs_0_ = bf16[384,1024]{1,0:T(8,128)(2,1)S(1)} collective-permute-done((bf16[384,1024]{1,0:T(8,128)(2,1)S(1)}, bf16[384,1024]{1,0:T(8,128)(2,1)S(1)}, u32[]{:S(2)}, u32[]{:S(2)}) %collective-permute-start.9) | collective-permute-done | bytes 786464 | tf_op jit(solution)/shard_map/ppermute | solution.py:176
  70.5 1.9 %attend_1.1 = (f32[384,512]{1,0:T(8,128)S(1)}, f32[384,512]{1,0:T(8,128)S(1)}, f32[384,512]{1,0:T(8,128)S(1)}) custom-call(s32[57]{0:T(128)S(1)} %pad_add_fusion.scal, bf16[384,512]{1,0:T(8,128)(2,1)S(1)} %copy-done, bf16[384,1024]{1,0:T(8,128)(2,1)S(1)} %collective-permute-done.9.refs_0_, f32[384,512]{1,0:T(8,128)S(1)} %get-tuple-element.26.refs_1_, ...), custom_call_target="tpu_custom_call" | custom-call | flops 301989888 | bytes 2359296 | tf_op jit(solution)/shard_map/attend_1/pallas_call | solution.py:151
  72.4 6.6 %collective-permute-done.6.refs_0_ = bf16[384,512]{1,0:T(8,128)(2,1)S(1)} collective-permute-done((bf16[384,512]{1,0:T(8,128)(2,1)S(1)}, bf16[384,512]{1,0:T(8,128)(2,1)S(1)}, u32[]{:S(2)}, u32[]{:S(2)}) %collective-permute-start.6) | collective-permute-done | bytes 393248 | tf_op jit(solution)/shard_map/ppermute | solution.py:176
  79.0 0.0 collective-permute-done.8.refs_3_
  79.0 2.6 %attend_3_2.1 = (f32[384,512]{1,0:T(8,128)S(1)}, f32[384,512]{1,0:T(8,128)S(1)}, f32[384,512]{1,0:T(8,128)S(1)}) custom-call(s32[57]{0:T(128)S(1)} %pad_add_fusion.scal, bf16[384,512]{1,0:T(8,128)(2,1)S(1)} %copy-done, bf16[384,512]{1,0:T(8,128)(2,1)S(1)} %collective-permute-done.6.refs_0_, bf16[384,512]{1,0:T(8,128)(2,1)S(1)} %collective-permute-done.7.refs_1_, ...), custom_call_target="tpu_custom_call" | custom-call | flops 603979776 | bytes 3538944 | tf_op jit(solution)/shard_map/attend_3_2/pallas_call | solution.py:151
  81.6 0.9 collective-permute-done.4.refs_1_
  82.5 10.1 %collective-permute-done.3.refs_0_ = bf16[384,1024]{1,0:T(8,128)(2,1)S(1)} collective-permute-done((bf16[384,1024]{1,0:T(8,128)(2,1)S(1)}, bf16[384,1024]{1,0:T(8,128)(2,1)S(1)}, u32[]{:S(2)}, u32[]{:S(2)}) %collective-permute-start.3) | collective-permute-done | bytes 786464 | tf_op jit(solution)/shard_map/ppermute | solution.py:212
  92.6 3.4 %attend_low_high.1 = bf16[384,512]{1,0:T(8,128)(2,1)} custom-call(s32[57]{0:T(128)S(1)} %pad_add_fusion.scal, bf16[384,512]{1,0:T(8,128)(2,1)S(1)} %copy-done, bf16[384,1024]{1,0:T(8,128)(2,1)S(1)} %collective-permute-done.3.refs_0_, bf16[384,1024]{1,0:T(8,128)(2,1)S(1)} %collective-permute-done.4.refs_1_, f32[384,512]{1,0:T(8,128)S(1)} %get-tuple-element.32.refs_2_, ...), custom_call_target="tpu_custom_call" | custom-call | flops 603979776 | bytes 2752512 | tf_op jit(solution)/shard_map/attend_low_high/pallas_call | solution.py:151
  (3 shorter events, 0.0 us)
Async XLA Ops:
  2.6 22.8 %copy-start = (bf16[384,512]{1,0:T(8,128)(2,1)S(1)}, bf16[384,512]{1,0:T(8,128)(2,1)}, u32[]{:S(2)}) copy-start(bf16[384,512]{1,0:T(8,128)(2,1)} %q_ref.9) | copy-start | bytes 1179652
  3.8 18.2 %collective-permute-start.2 = (bf16[384,1024]{1,0:T(8,128)(2,1)S(1)}, bf16[384,1024]{1,0:T(8,128)(2,1)}, u32[]{:S(2)}, u32[]{:S(2)}) collective-permute-start(bf16[384,1024]{1,0:T(8,128)(2,1)S(1)} %pad_maximum_fusion.refs_0_), channel_id=1, source_target_pairs={{0,8},{8,0},{16,24},{24,16},{32,40},{40,32},{48,56},{56,48},{64,72... | collective-permute-start | bytes 2359304 | tf_op jit(solution)/shard_map/ppermute | solution.py:176
  5.8 36.8 %collective-permute-start.1 = (bf16[384,1024]{1,0:T(8,128)(2,1)S(1)}, bf16[384,1024]{1,0:T(8,128)(2,1)S(1)}, u32[]{:S(2)}, u32[]{:S(2)}) collective-permute-start(bf16[384,1024]{1,0:T(8,128)(2,1)S(1)} %pad_maximum_fusion.refs_0_), channel_id=1, source_target_pairs={{0,256},{8,264},{16,272},{24,280},{32,288},{40,296},{48,304},{56,3... | collective-permute-start | bytes 2359304 | tf_op jit(solution)/shard_map/ppermute | solution.py:176
  8.2 37.3 %collective-permute-start = (bf16[384,1024]{1,0:T(8,128)(2,1)S(1)}, bf16[384,1024]{1,0:T(8,128)(2,1)S(1)}, u32[]{:S(2)}, u32[]{:S(2)}) collective-permute-start(bf16[384,1024]{1,0:T(8,128)(2,1)S(1)} %pad_maximum_fusion.refs_0_), channel_id=1, source_target_pairs={{0,128},{8,136},{16,144},{24,152},{32,160},{40,168},{48,176},{56,1... | collective-permute-start | bytes 2359304 | tf_op jit(solution)/shard_map/ppermute | solution.py:176
  11.6 39.8 %collective-permute-start.5 = (bf16[384,512]{1,0:T(8,128)(2,1)}, bf16[384,512]{1,0:T(8,128)(2,1)S(1)}, u32[]{:S(2)}, u32[]{:S(2)}) collective-permute-start(bf16[384,512]{1,0:T(8,128)(2,1)} %fusion), channel_id=1, source_target_pairs={{0,32},{8,40},{16,48},{24,56},{32,0},{40,8},{48,16},{56,24},{64,96... | collective-permute-start | bytes 1179656 | tf_op jit(solution)/shard_map/ppermute | solution.py:176
  16.1 35.3 %collective-permute-start.7 = (bf16[384,512]{1,0:T(8,128)(2,1)}, bf16[384,512]{1,0:T(8,128)(2,1)S(1)}, u32[]{:S(2)}, u32[]{:S(2)}) collective-permute-start(bf16[384,512]{1,0:T(8,128)(2,1)} %param.7), channel_id=1, source_target_pairs={{0,64},{8,72},{16,80},{24,88},{32,96},{40,104},{48,112},{56,120},{... | collective-permute-start | bytes 1179656 | tf_op jit(solution)/shard_map/ppermute | solution.py:176
  22.1 48.4 %collective-permute-start.9 = (bf16[384,1024]{1,0:T(8,128)(2,1)S(1)}, bf16[384,1024]{1,0:T(8,128)(2,1)S(1)}, u32[]{:S(2)}, u32[]{:S(2)}) collective-permute-start(bf16[384,1024]{1,0:T(8,128)(2,1)S(1)} %pad_maximum_fusion.refs_0_), channel_id=1, source_target_pairs={{0,16},{8,24},{16,0},{24,8},{32,48},{40,56},{48,32},{56,40},{64,80... | collective-permute-start | bytes 2359304 | tf_op jit(solution)/shard_map/ppermute | solution.py:176
  45.5 37.0 %collective-permute-start.4 = (bf16[384,1024]{1,0:T(8,128)(2,1)S(1)}, bf16[384,1024]{1,0:T(8,128)(2,1)S(1)}, u32[]{:S(2)}, u32[]{:S(2)}) collective-permute-start(bf16[384,1024]{1,0:T(8,128)(2,1)S(1)} %pad_maximum_fusion.refs_0_), channel_id=1, source_target_pairs={{1,0},{2,1},{3,2},{4,3},{5,4},{6,5},{7,6},{9,8},{10,9},{11,10},{12... | collective-permute-start | bytes 2359304 | tf_op jit(solution)/shard_map/ppermute | solution.py:213
  49.0 43.6 %collective-permute-start.3 = (bf16[384,1024]{1,0:T(8,128)(2,1)S(1)}, bf16[384,1024]{1,0:T(8,128)(2,1)S(1)}, u32[]{:S(2)}, u32[]{:S(2)}) collective-permute-start(bf16[384,1024]{1,0:T(8,128)(2,1)S(1)} %pad_maximum_fusion.refs_0_), channel_id=1, source_target_pairs={{0,1},{1,2},{2,3},{3,4},{4,5},{5,6},{6,7},{8,9},{9,10},{10,11},{11... | collective-permute-start | bytes 2359304 | tf_op jit(solution)/shard_map/ppermute | solution.py:212
  51.4 27.6 %collective-permute-start.6 = (bf16[384,512]{1,0:T(8,128)(2,1)S(1)}, bf16[384,512]{1,0:T(8,128)(2,1)S(1)}, u32[]{:S(2)}, u32[]{:S(2)}) collective-permute-start(bf16[384,512]{1,0:T(8,128)(2,1)S(1)} %collective-permute-done.5.refs_2_), channel_id=1, source_target_pairs={{0,96},{8,104},{16,112},{24,120},{32,64},{40,72},{48,80},{56,88},{... | collective-permute-start | bytes 1179656 | tf_op jit(solution)/shard_map/ppermute | solution.py:176
  56.7 22.3 %collective-permute-start.8 = (bf16[384,512]{1,0:T(8,128)(2,1)}, bf16[384,512]{1,0:T(8,128)(2,1)S(1)}, u32[]{:S(2)}, u32[]{:S(2)}) collective-permute-start(bf16[384,512]{1,0:T(8,128)(2,1)} %param.7), channel_id=1, source_target_pairs={{0,32},{8,40},{16,48},{24,56},{32,0},{40,8},{48,16},{56,24},{64,96... | collective-permute-start | bytes 1179656 | tf_op jit(solution)/shard_map/ppermute | solution.py:176

commit v4 on v3

--- a/solution.py
+++ b/solution.py
@@ -11,6 +11,7 @@
 BLK = 128
 LOG2E = 1.4426950408889634
 NEG = -1e30
+TM = ("b5", "b4", "b3", "b2", "b1", "b0")
 
 
 def attend_kernel(kinds, packed, first, last, heads, scal, q_ref, *refs):
@@ -20,6 +21,8 @@
     for whole in packed:
         if whole:
             kv = refs.pop(0)
+            if len(kv.shape) == 3:
+                kv = kv.at[scal[3]]
             tiles.append((kv, kv, width))
         else:
             tiles.append((refs.pop(0), refs.pop(0), 0))
@@ -55,7 +58,7 @@
             elif kind == "high":
                 gates = [scal[2]] * blocks
             else:
-                base = 3 + (qb * 6 + kind) * blocks
+                base = 4 + (qb * 6 + kind) * blocks
                 gates = [scal[base + kb] for kb in range(blocks)]
             row = []
             for kb in range(blocks):
@@ -167,13 +170,13 @@
 
 def per_device(queries, keys, values, block_mask, tile_counts):
     rows, width = queries.shape
-    tm_size = lax.axis_size("tm")
+    tm_size = lax.axis_size(TM)
     space_size = lax.axis_size("space")
     space_index = lax.axis_index("space")
     count = tile_counts.reshape(())
 
     def partner(value, mask):
-        return lax.ppermute(value, "tm", [(i, i ^ mask) for i in range(tm_size)])
+        return lax.ppermute(value, TM, [(i, i ^ mask) for i in range(tm_size)])
 
     scal = jnp.concatenate(
         [
@@ -182,6 +185,7 @@
                     count,
                     (space_index > 0).astype(jnp.int32),
                     (space_index < space_size - 1).astype(jnp.int32),
+                    1 - lax.axis_index("b0"),
                 ]
             ),
             block_mask.reshape(-1),
@@ -204,27 +208,32 @@
     y1 = partner(both, 2)
     z2 = partner(both, 32)
     z1 = partner(both, 16)
-    core = partner(both, 1)
-    state = attend(scal, queries, [("own", both), (0, core)], None, False)
+    state = attend(scal, queries, [("own", both)], None, False)
+    own = after(both, state[0])
+    core = lax.all_to_all(jnp.stack([own, own]), "b0", 0, 0)
     y4_k = partner(after(y2_k, state[0]), 12)
     y2_v = partner(after(values, y2_k, y4_v, state[0]), 4)
-    second = after(both, z1, z2, state[0])
+    second = after(both, z1, z2, state[0], core)
     low = lax.ppermute(second, "space", up)
     high = lax.ppermute(second, "space", down)
-    state = attend(scal, queries, [(4, z1), (5, z2)], state, False)
+    state = attend(scal, queries, [(4, z1), (5, z2), (0, core)], state, False)
     state = attend(scal, queries, [(1, y1)], state, False)
     state = attend(scal, queries, [(3, y4_k, y4_v), (2, y2_k, y2_v)], state, False)
     return attend(scal, queries, [("low", low), ("high", high)], state, True)
 
 
 def solution(mesh):
+    bits = jax.sharding.Mesh(
+        mesh.devices.reshape((2,) * len(TM) + (mesh.shape["space"],)), TM + ("space",)
+    )
+    rows = TM + ("space",)
     placed = (
-        P(("tm", "space"), None),
-        P(("tm", "space"), None),
-        P(("tm", "space"), None),
-        P(("tm", "space"), None, None),
-        P("tm", "space"),
+        P(rows, None),
+        P(rows, None),
+        P(rows, None),
+        P(rows, None, None),
+        P(TM, "space"),
     )
     return jax.shard_map(
-        per_device, mesh=mesh, in_specs=placed, out_specs=P(("tm", "space"), None), check_vma=False
-    )
+        per_device, mesh=bits, in_specs=placed, out_specs=P(rows, None), check_vma=False
+    )

time: 96.5 us -> 92.8 us (0.962)
  the two profiles are of different devices: /device:TPU:392 before, /device:TPU:440 now
where the time goes in v4:
time: 92.8 us; the launch traced here: 92.4 us
  waiting for transfers between devices  40.8 us (44%)
  starting transfers between devices  28.2 us (30%)
  Pallas kernels  13.3 us (14%)
  blocking collectives  5 us (5%)
  other arithmetic  3.24 us (3%)
  local copies, waits for them, and re-layouts  0.97 us (1%)
    ppermute x7, waiting for transfers between devices, partner(): return lax.ppermute(value, TM, [(i, i ^ mask) for i in range(tm_size)])  32.4 us
    ppermute x7, starting transfers between devices, partner(): return lax.ppermute(value, TM, [(i, i ^ mask) for i in range(tm_size)])  22.3 us
    pallas_call x5, Pallas kernels, attend(): pl.pallas_call(functools.partial(attend_kernel, kinds, packed, first, las...  13.3 us
    ppermute x1, waiting for transfers between devices, per_device(): low = lax.ppermute(second, 'space', up)  8.41 us
    all_to_all x1, blocking collectives, per_device(): core = lax.all_to_all(jnp.stack([own, own]), 'b0', 0, 0)  5 us
    ppermute x1, starting transfers between devices, per_device(): high = lax.ppermute(second, 'space', down)  3.46 us
    ppermute x1, starting transfers between devices, per_device(): low = lax.ppermute(second, 'space', up)  2.37 us
    select_n x1, other arithmetic, per_device(): marked = jnp.where((row == rows - 1) & (count < rows), code, keys)  1.9 us
  transfers between devices with their start and end apart: 9, of which 5 were waited for; matrix products, arithmetic and copies ran while one was open for 1% of the time, Pallas kernels for 11%

profile of v4, /device:TPU:440, one launch (start us, length us, event | category | flops | bytes accessed | tf_op | source)
XLA Modules:
  0.0 92.4 jit_solution(2512789286201154930)
XLA Ops:
  0.0 0.0 copy-start
  0.7 1.9 %fusion = bf16[384,512]{1,0:T(8,128)(2,1)} fusion(bf16[384,512]{1,0:T(8,128)(2,1)} %param.6, s32[]{:T(128)} %bitcast.6, s32[]{:T(128)} %bitcast.5, s32[512]{0:T(512)S(1)} %get-tuple-element.37, s32[512]{0:T(512)S(1)} %get-tuple-element.38, pred[384]{0:T(512)(128)(4,1)S(1)} %fusion.4, pred[512]{0:T(512)(128)(4,1)S(1)} %fusion.3), kind=kLoop, calls=%fused_computation.5 | loop fusion | flops 1572864 | bytes 791432 | tf_op jit(solution)/shard_map/jit(_where)/select_n | solution.py:201
  2.6 1.2 %pad_maximum_fusion.1.refs_0_ = bf16[384,1024]{1,0:T(8,128)(2,1)S(1)} fusion(bf16[384,512]{1,0:T(8,128)(2,1)} %param.7, bf16[384,512]{1,0:T(8,128)(2,1)} %fusion), kind=kLoop, calls=%fused_computation.3 | loop fusion | flops 1572864 | bytes 1572864 | tf_op jit(solution)/shard_map/concatenate | solution.py:205
  3.8 2.5 %collective-permute-start.1 = (bf16[384,1024]{1,0:T(8,128)(2,1)S(1)}, bf16[384,1024]{1,0:T(8,128)(2,1)S(1)}, u32[]{:S(2)}, u32[]{:S(2)}) collective-permute-start(bf16[384,1024]{1,0:T(8,128)(2,1)S(1)} %pad_maximum_fusion.1.refs_0_), channel_id=1, source_target_pairs={{0,256},{8,264},{16,272},{24,280},{32,288},{40,296},{48,304},{56,3... | collective-permute-start | bytes 2359304 | tf_op jit(solution)/shard_map/ppermute | solution.py:179
  6.3 3.4 %collective-permute-start = (bf16[384,1024]{1,0:T(8,128)(2,1)S(1)}, bf16[384,1024]{1,0:T(8,128)(2,1)S(1)}, u32[]{:S(2)}, u32[]{:S(2)}) collective-permute-start(bf16[384,1024]{1,0:T(8,128)(2,1)S(1)} %pad_maximum_fusion.1.refs_0_), channel_id=1, source_target_pairs={{0,128},{8,136},{16,144},{24,152},{32,160},{40,168},{48,176},{56,1... | collective-permute-start | bytes 2359304 | tf_op jit(solution)/shard_map/ppermute | solution.py:179
  9.7 4.0 %collective-permute-start.4 = (bf16[384,512]{1,0:T(8,128)(2,1)}, bf16[384,512]{1,0:T(8,128)(2,1)}, u32[]{:S(2)}, u32[]{:S(2)}) collective-permute-start(bf16[384,512]{1,0:T(8,128)(2,1)} %fusion), channel_id=1, source_target_pairs={{0,32},{8,40},{16,48},{24,56},{32,0},{40,8},{48,16},{56,24},{64,96... | collective-permute-start | bytes 1179656 | tf_op jit(solution)/shard_map/ppermute | solution.py:179
  13.7 2.9 %collective-permute-start.6 = (bf16[384,512]{1,0:T(8,128)(2,1)}, bf16[384,512]{1,0:T(8,128)(2,1)}, u32[]{:S(2)}, u32[]{:S(2)}) collective-permute-start(bf16[384,512]{1,0:T(8,128)(2,1)} %param.7), channel_id=1, source_target_pairs={{0,64},{8,72},{16,80},{24,88},{32,96},{40,104},{48,112},{56,120},{... | collective-permute-start | bytes 1179656 | tf_op jit(solution)/shard_map/ppermute | solution.py:179
  16.7 2.4 %collective-permute-start.8 = (bf16[384,1024]{1,0:T(8,128)(2,1)S(1)}, bf16[384,1024]{1,0:T(8,128)(2,1)S(1)}, u32[]{:S(2)}, u32[]{:S(2)}) collective-permute-start(bf16[384,1024]{1,0:T(8,128)(2,1)S(1)} %pad_maximum_fusion.1.refs_0_), channel_id=1, source_target_pairs={{0,16},{8,24},{16,0},{24,8},{32,48},{40,56},{48,32},{56,40},{64,80... | collective-permute-start | bytes 2359304 | tf_op jit(solution)/shard_map/ppermute | solution.py:179
  19.0 0.8 copy.7
  19.8 0.1 reshape.10
  19.9 0.1 concatenate.6.scal
  20.0 0.0 copy-done
  20.0 1.8 %attend_own.1 = (f32[384,512]{1,0:T(8,128)S(1)}, f32[384,512]{1,0:T(8,128)S(1)}, f32[384,512]{1,0:T(8,128)S(1)}) custom-call(s32[58]{0:T(128)S(1)} %concatenate.6.scal, bf16[384,512]{1,0:T(8,128)(2,1)S(1)} %copy-done, bf16[384,1024]{1,0:T(8,128)(2,1)S(1)} %pad_maximum_fusion.1.refs_0_), custom_call_target="tpu_custom_call" | custom-call | flops 301989888 | bytes 1179648 | tf_op jit(solution)/shard_map/attend_own/pallas_call | solution.py:154
  21.8 0.1 pad_maximum_fusion
  22.0 5.0 %all_to_all.5.refs_2_ = bf16[2,384,1024]{2,1,0:T(8,128)(2,1)S(1)} all-to-all(bf16[2,384,1024]{2,1,0:T(8,128)(2,1)S(1)} %pad_maximum_fusion), channel_id=1, replica_groups=mesh['b5'=2,'b4'=2,'b3'=2,'b2'=2,'b1'=2,'b0'=2,'space'=8] {'b0'}, dimensions={0} | all-to-all | bytes 3145728 | tf_op jit(solution)/shard_map/all_to_all | solution.py:213
  27.0 13.0 %collective-permute-done.1.refs_1_ = bf16[384,1024]{1,0:T(8,128)(2,1)S(1)} collective-permute-done((bf16[384,1024]{1,0:T(8,128)(2,1)S(1)}, bf16[384,1024]{1,0:T(8,128)(2,1)S(1)}, u32[]{:S(2)}, u32[]{:S(2)}) %collective-permute-start.1) | collective-permute-done | bytes 786464 | tf_op jit(solution)/shard_map/ppermute | solution.py:179
  40.0 3.0 %collective-permute-done.refs_0_ = bf16[384,1024]{1,0:T(8,128)(2,1)S(1)} collective-permute-done((bf16[384,1024]{1,0:T(8,128)(2,1)S(1)}, bf16[384,1024]{1,0:T(8,128)(2,1)S(1)}, u32[]{:S(2)}, u32[]{:S(2)}) %collective-permute-start) | collective-permute-done | bytes 786464 | tf_op jit(solution)/shard_map/ppermute | solution.py:179
  42.9 3.5 %collective-permute-start.3 = (bf16[384,1024]{1,0:T(8,128)(2,1)S(1)}, bf16[384,1024]{1,0:T(8,128)(2,1)S(1)}, u32[]{:S(2)}, u32[]{:S(2)}) collective-permute-start(bf16[384,1024]{1,0:T(8,128)(2,1)S(1)} %pad_maximum_fusion.1.refs_0_), channel_id=1, source_target_pairs={{1,0},{2,1},{3,2},{4,3},{5,4},{6,5},{7,6},{9,8},{10,9},{11,10},{12... | collective-permute-start | bytes 2359304 | tf_op jit(solution)/shard_map/ppermute | solution.py:218
  46.4 2.4 %collective-permute-start.2 = (bf16[384,1024]{1,0:T(8,128)(2,1)S(1)}, bf16[384,1024]{1,0:T(8,128)(2,1)S(1)}, u32[]{:S(2)}, u32[]{:S(2)}) collective-permute-start(bf16[384,1024]{1,0:T(8,128)(2,1)S(1)} %pad_maximum_fusion.1.refs_0_), channel_id=1, source_target_pairs={{0,1},{1,2},{2,3},{3,4},{4,5},{5,6},{6,7},{8,9},{9,10},{10,11},{11... | collective-permute-start | bytes 2359304 | tf_op jit(solution)/shard_map/ppermute | solution.py:217
  48.8 0.0 collective-permute-done.4.refs_2_
  48.8 0.0 collective-permute-done.6.refs_1_
  48.8 2.7 %collective-permute-start.5 = (bf16[384,512]{1,0:T(8,128)(2,1)}, bf16[384,512]{1,0:T(8,128)(2,1)S(1)}, u32[]{:S(2)}, u32[]{:S(2)}) collective-permute-start(bf16[384,512]{1,0:T(8,128)(2,1)} %collective-permute-done.4.refs_2_), channel_id=1, source_target_pairs={{0,96},{8,104},{16,112},{24,120},{32,64},{40,72},{48,80},{56,88},{... | collective-permute-start | bytes 1179656 | tf_op jit(solution)/shard_map/ppermute | solution.py:179
  51.5 4.5 %collective-permute-start.7 = (bf16[384,512]{1,0:T(8,128)(2,1)}, bf16[384,512]{1,0:T(8,128)(2,1)S(1)}, u32[]{:S(2)}, u32[]{:S(2)}) collective-permute-start(bf16[384,512]{1,0:T(8,128)(2,1)} %param.7), channel_id=1, source_target_pairs={{0,32},{8,40},{16,48},{24,56},{32,0},{40,8},{48,16},{56,24},{64,96... | collective-permute-start | bytes 1179656 | tf_op jit(solution)/shard_map/ppermute | solution.py:179
  56.0 3.3 %attend_4_5_0.1 = (f32[384,512]{1,0:T(8,128)S(1)}, f32[384,512]{1,0:T(8,128)S(1)}, f32[384,512]{1,0:T(8,128)S(1)}) custom-call(s32[58]{0:T(128)S(1)} %concatenate.6.scal, bf16[384,512]{1,0:T(8,128)(2,1)S(1)} %copy-done, bf16[384,1024]{1,0:T(8,128)(2,1)S(1)} %collective-permute-done.refs_0_, bf16[384,1024]{1,0:T(8,128)(2,1)S(1)} %collective-permute-done.1.refs_1_, ...), custom_call_target="tpu_custom_call" | custom-call | flops 905969664 | bytes 3145728 | tf_op jit(solution)/shard_map/attend_4_5_0/pallas_call | solution.py:154
  59.3 9.2 %collective-permute-done.8.refs_0_ = bf16[384,1024]{1,0:T(8,128)(2,1)S(1)} collective-permute-done((bf16[384,1024]{1,0:T(8,128)(2,1)S(1)}, bf16[384,1024]{1,0:T(8,128)(2,1)S(1)}, u32[]{:S(2)}, u32[]{:S(2)}) %collective-permute-start.8) | collective-permute-done | bytes 786464 | tf_op jit(solution)/shard_map/ppermute | solution.py:179
  68.6 1.9 %attend_1.1 = (f32[384,512]{1,0:T(8,128)S(1)}, f32[384,512]{1,0:T(8,128)S(1)}, f32[384,512]{1,0:T(8,128)S(1)}) custom-call(s32[58]{0:T(128)S(1)} %concatenate.6.scal, bf16[384,512]{1,0:T(8,128)(2,1)S(1)} %copy-done, bf16[384,1024]{1,0:T(8,128)(2,1)S(1)} %collective-permute-done.8.refs_0_, f32[384,512]{1,0:T(8,128)S(1)} %get-tuple-element.28.refs_1_, ...), custom_call_target="tpu_custom_call" | custom-call | flops 301989888 | bytes 2359296 | tf_op jit(solution)/shard_map/attend_1/pallas_call | solution.py:154
  70.5 7.2 %collective-permute-done.5.refs_0_ = bf16[384,512]{1,0:T(8,128)(2,1)S(1)} collective-permute-done((bf16[384,512]{1,0:T(8,128)(2,1)}, bf16[384,512]{1,0:T(8,128)(2,1)S(1)}, u32[]{:S(2)}, u32[]{:S(2)}) %collective-permute-start.5) | collective-permute-done | bytes 393248 | tf_op jit(solution)/shard_map/ppermute | solution.py:179
  77.6 0.0 collective-permute-done.7.refs_3_
  77.6 3.1 %attend_3_2.1 = (f32[384,512]{1,0:T(8,128)S(1)}, f32[384,512]{1,0:T(8,128)S(1)}, f32[384,512]{1,0:T(8,128)S(1)}) custom-call(s32[58]{0:T(128)S(1)} %concatenate.6.scal, bf16[384,512]{1,0:T(8,128)(2,1)S(1)} %copy-done, bf16[384,512]{1,0:T(8,128)(2,1)S(1)} %collective-permute-done.5.refs_0_, bf16[384,512]{1,0:T(8,128)(2,1)} %collective-permute-done.6.refs_1_, ...), custom_call_target="tpu_custom_call" | custom-call | flops 603979776 | bytes 3538944 | tf_op jit(solution)/shard_map/attend_3_2/pallas_call | solution.py:154
  80.7 0.0 collective-permute-done.3.refs_1_
  80.7 8.4 %collective-permute-done.2.refs_0_ = bf16[384,1024]{1,0:T(8,128)(2,1)S(1)} collective-permute-done((bf16[384,1024]{1,0:T(8,128)(2,1)S(1)}, bf16[384,1024]{1,0:T(8,128)(2,1)S(1)}, u32[]{:S(2)}, u32[]{:S(2)}) %collective-permute-start.2) | collective-permute-done | bytes 786464 | tf_op jit(solution)/shard_map/ppermute | solution.py:217
  89.2 3.2 %attend_low_high.1 = bf16[384,512]{1,0:T(8,128)(2,1)} custom-call(s32[58]{0:T(128)S(1)} %concatenate.6.scal, bf16[384,512]{1,0:T(8,128)(2,1)S(1)} %copy-done, bf16[384,1024]{1,0:T(8,128)(2,1)S(1)} %collective-permute-done.2.refs_0_, bf16[384,1024]{1,0:T(8,128)(2,1)S(1)} %collective-permute-done.3.refs_1_, f32[384,512]{1,0:T(8,128)S(1)} %get-tuple-element.34.refs_2_, ...), custom_call_target="tpu_custom_call" | custom-call | flops 603979776 | bytes 2752512 | tf_op jit(solution)/shard_map/attend_low_high/pallas_call | solution.py:154
  (3 shorter events, 0.0 us)
Async XLA Ops:
  0.0 20.0 %copy-start = (bf16[384,512]{1,0:T(8,128)(2,1)S(1)}, bf16[384,512]{1,0:T(8,128)(2,1)}, u32[]{:S(2)}) copy-start(bf16[384,512]{1,0:T(8,128)(2,1)} %q_ref.9) | copy-start | bytes 1179652
  3.8 36.1 %collective-permute-start.1 = (bf16[384,1024]{1,0:T(8,128)(2,1)S(1)}, bf16[384,1024]{1,0:T(8,128)(2,1)S(1)}, u32[]{:S(2)}, u32[]{:S(2)}) collective-permute-start(bf16[384,1024]{1,0:T(8,128)(2,1)S(1)} %pad_maximum_fusion.1.refs_0_), channel_id=1, source_target_pairs={{0,256},{8,264},{16,272},{24,280},{32,288},{40,296},{48,304},{56,3... | collective-permute-start | bytes 2359304 | tf_op jit(solution)/shard_map/ppermute | solution.py:179
  6.3 36.6 %collective-permute-start = (bf16[384,1024]{1,0:T(8,128)(2,1)S(1)}, bf16[384,1024]{1,0:T(8,128)(2,1)S(1)}, u32[]{:S(2)}, u32[]{:S(2)}) collective-permute-start(bf16[384,1024]{1,0:T(8,128)(2,1)S(1)} %pad_maximum_fusion.1.refs_0_), channel_id=1, source_target_pairs={{0,128},{8,136},{16,144},{24,152},{32,160},{40,168},{48,176},{56,1... | collective-permute-start | bytes 2359304 | tf_op jit(solution)/shard_map/ppermute | solution.py:179
  9.7 39.1 %collective-permute-start.4 = (bf16[384,512]{1,0:T(8,128)(2,1)}, bf16[384,512]{1,0:T(8,128)(2,1)}, u32[]{:S(2)}, u32[]{:S(2)}) collective-permute-start(bf16[384,512]{1,0:T(8,128)(2,1)} %fusion), channel_id=1, source_target_pairs={{0,32},{8,40},{16,48},{24,56},{32,0},{40,8},{48,16},{56,24},{64,96... | collective-permute-start | bytes 1179656 | tf_op jit(solution)/shard_map/ppermute | solution.py:179
  13.7 35.1 %collective-permute-start.6 = (bf16[384,512]{1,0:T(8,128)(2,1)}, bf16[384,512]{1,0:T(8,128)(2,1)}, u32[]{:S(2)}, u32[]{:S(2)}) collective-permute-start(bf16[384,512]{1,0:T(8,128)(2,1)} %param.7), channel_id=1, source_target_pairs={{0,64},{8,72},{16,80},{24,88},{32,96},{40,104},{48,112},{56,120},{... | collective-permute-start | bytes 1179656 | tf_op jit(solution)/shard_map/ppermute | solution.py:179
  16.7 51.9 %collective-permute-start.8 = (bf16[384,1024]{1,0:T(8,128)(2,1)S(1)}, bf16[384,1024]{1,0:T(8,128)(2,1)S(1)}, u32[]{:S(2)}, u32[]{:S(2)}) collective-permute-start(bf16[384,1024]{1,0:T(8,128)(2,1)S(1)} %pad_maximum_fusion.1.refs_0_), channel_id=1, source_target_pairs={{0,16},{8,24},{16,0},{24,8},{32,48},{40,56},{48,32},{56,40},{64,80... | collective-permute-start | bytes 2359304 | tf_op jit(solution)/shard_map/ppermute | solution.py:179
  42.9 37.8 %collective-permute-start.3 = (bf16[384,1024]{1,0:T(8,128)(2,1)S(1)}, bf16[384,1024]{1,0:T(8,128)(2,1)S(1)}, u32[]{:S(2)}, u32[]{:S(2)}) collective-permute-start(bf16[384,1024]{1,0:T(8,128)(2,1)S(1)} %pad_maximum_fusion.1.refs_0_), channel_id=1, source_target_pairs={{1,0},{2,1},{3,2},{4,3},{5,4},{6,5},{7,6},{9,8},{10,9},{11,10},{12... | collective-permute-start | bytes 2359304 | tf_op jit(solution)/shard_map/ppermute | solution.py:218
  46.4 42.8 %collective-permute-start.2 = (bf16[384,1024]{1,0:T(8,128)(2,1)S(1)}, bf16[384,1024]{1,0:T(8,128)(2,1)S(1)}, u32[]{:S(2)}, u32[]{:S(2)}) collective-permute-start(bf16[384,1024]{1,0:T(8,128)(2,1)S(1)} %pad_maximum_fusion.1.refs_0_), channel_id=1, source_target_pairs={{0,1},{1,2},{2,3},{3,4},{4,5},{5,6},{6,7},{8,9},{9,10},{10,11},{11... | collective-permute-start | bytes 2359304 | tf_op jit(solution)/shard_map/ppermute | solution.py:217
  48.8 28.8 %collective-permute-start.5 = (bf16[384,512]{1,0:T(8,128)(2,1)}, bf16[384,512]{1,0:T(8,128)(2,1)S(1)}, u32[]{:S(2)}, u32[]{:S(2)}) collective-permute-start(bf16[384,512]{1,0:T(8,128)(2,1)} %collective-permute-done.4.refs_2_), channel_id=1, source_target_pairs={{0,96},{8,104},{16,112},{24,120},{32,64},{40,72},{48,80},{56,88},{... | collective-permute-start | bytes 1179656 | tf_op jit(solution)/shard_map/ppermute | solution.py:179
  51.5 26.1 %collective-permute-start.7 = (bf16[384,512]{1,0:T(8,128)(2,1)}, bf16[384,512]{1,0:T(8,128)(2,1)S(1)}, u32[]{:S(2)}, u32[]{:S(2)}) collective-permute-start(bf16[384,512]{1,0:T(8,128)(2,1)} %param.7), channel_id=1, source_target_pairs={{0,32},{8,40},{16,48},{24,56},{32,0},{40,8},{48,16},{56,24},{64,96... | collective-permute-start | bytes 1179656 | tf_op jit(solution)/shard_map/ppermute | solution.py:179

commit v5 on v4

--- a/solution.py
+++ b/solution.py
@@ -213,13 +213,14 @@
     core = lax.all_to_all(jnp.stack([own, own]), "b0", 0, 0)
     y4_k = partner(after(y2_k, state[0]), 12)
     y2_v = partner(after(values, y2_k, y4_v, state[0]), 4)
-    second = after(both, z1, z2, state[0], core)
+    second = after(both, z2, z1, state[0], core)
     low = lax.ppermute(second, "space", up)
     high = lax.ppermute(second, "space", down)
-    state = attend(scal, queries, [(4, z1), (5, z2), (0, core)], state, False)
+    state = attend(scal, queries, [(5, z2), (4, z1), (0, core)], state, False)
     state = attend(scal, queries, [(1, y1)], state, False)
-    state = attend(scal, queries, [(3, y4_k, y4_v), (2, y2_k, y2_v)], state, False)
-    return attend(scal, queries, [("low", low), ("high", high)], state, True)
+    state = attend(scal, queries, [(3, y4_k, y4_v)], state, False)
+    state = attend(scal, queries, [(2, y2_k, y2_v)], state, False)
+    return attend(scal, queries, [("high", high), ("low", low)], state, True)
 
 
 def solution(mesh):

time: 92.8 us -> 92.9 us (level)
  the two profiles are of different devices: /device:TPU:440 before, /device:TPU:392 now
where the time goes in v5:
time: 92.9 us; the launch traced here: 92.4 us
  waiting for transfers between devices  35.7 us (38%)
  starting transfers between devices  31.6 us (34%)
  Pallas kernels  14.9 us (16%)
  blocking collectives  5 us (5%)
  other arithmetic  3.24 us (3%)
  local copies, waits for them, and re-layouts  0.97 us (1%)
    ppermute x7, waiting for transfers between devices, partner(): return lax.ppermute(value, TM, [(i, i ^ mask) for i in range(tm_size)])  29.1 us
    ppermute x7, starting transfers between devices, partner(): return lax.ppermute(value, TM, [(i, i ^ mask) for i in range(tm_size)])  25.8 us
    pallas_call x6, Pallas kernels, attend(): pl.pallas_call(functools.partial(attend_kernel, kinds, packed, first, las...  14.9 us
    ppermute x1, waiting for transfers between devices, per_device(): low = lax.ppermute(second, 'space', up)  6.63 us
    all_to_all x1, blocking collectives, per_device(): core = lax.all_to_all(jnp.stack([own, own]), 'b0', 0, 0)  5 us
    ppermute x1, starting transfers between devices, per_device(): high = lax.ppermute(second, 'space', down)  3.46 us
    ppermute x1, starting transfers between devices, per_device(): low = lax.ppermute(second, 'space', up)  2.37 us
    select_n x1, other arithmetic, per_device(): marked = jnp.where((row == rows - 1) & (count < rows), code, keys)  1.89 us
  transfers between devices with their start and end apart: 9, of which 6 were waited for; matrix products, arithmetic and copies ran while one was open for 1% of the time, Pallas kernels for 13%

profile of v5, /device:TPU:392, one launch (start us, length us, event | category | flops | bytes accessed | tf_op | source)
XLA Modules:
  0.0 92.4 jit_solution(6772754255633372631)
XLA Ops:
  0.7 1.9 %fusion = bf16[384,512]{1,0:T(8,128)(2,1)} fusion(bf16[384,512]{1,0:T(8,128)(2,1)} %param.6, s32[]{:T(128)} %bitcast.6, s32[]{:T(128)} %bitcast.5, s32[512]{0:T(512)S(1)} %get-tuple-element.43, s32[512]{0:T(512)S(1)} %get-tuple-element.44, pred[384]{0:T(512)(128)(4,1)S(1)} %fusion.4, pred[512]{0:T(512)(128)(4,1)S(1)} %fusion.3), kind=kLoop, calls=%fused_computation.5 | loop fusion | flops 1572864 | bytes 791432 | tf_op jit(solution)/shard_map/jit(_where)/select_n | solution.py:201
  2.6 1.2 %pad_maximum_fusion.1.refs_0_ = bf16[384,1024]{1,0:T(8,128)(2,1)S(1)} fusion(bf16[384,512]{1,0:T(8,128)(2,1)} %param.7, bf16[384,512]{1,0:T(8,128)(2,1)} %fusion), kind=kLoop, calls=%fused_computation.3 | loop fusion | flops 1572864 | bytes 1572864 | tf_op jit(solution)/shard_map/concatenate | solution.py:205
  3.8 2.5 %collective-permute-start = (bf16[384,1024]{1,0:T(8,128)(2,1)S(1)}, bf16[384,1024]{1,0:T(8,128)(2,1)S(1)}, u32[]{:S(2)}, u32[]{:S(2)}) collective-permute-start(bf16[384,1024]{1,0:T(8,128)(2,1)S(1)} %pad_maximum_fusion.1.refs_0_), channel_id=1, source_target_pairs={{0,256},{8,264},{16,272},{24,280},{32,288},{40,296},{48,304},{56,3... | collective-permute-start | bytes 2359304 | tf_op jit(solution)/shard_map/ppermute | solution.py:179
  6.3 3.4 %collective-permute-start.1 = (bf16[384,1024]{1,0:T(8,128)(2,1)S(1)}, bf16[384,1024]{1,0:T(8,128)(2,1)S(1)}, u32[]{:S(2)}, u32[]{:S(2)}) collective-permute-start(bf16[384,1024]{1,0:T(8,128)(2,1)S(1)} %pad_maximum_fusion.1.refs_0_), channel_id=1, source_target_pairs={{0,128},{8,136},{16,144},{24,152},{32,160},{40,168},{48,176},{56,1... | collective-permute-start | bytes 2359304 | tf_op jit(solution)/shard_map/ppermute | solution.py:179
  9.7 2.4 %collective-permute-start.8 = (bf16[384,1024]{1,0:T(8,128)(2,1)S(1)}, bf16[384,1024]{1,0:T(8,128)(2,1)S(1)}, u32[]{:S(2)}, u32[]{:S(2)}) collective-permute-start(bf16[384,1024]{1,0:T(8,128)(2,1)S(1)} %pad_maximum_fusion.1.refs_0_), channel_id=1, source_target_pairs={{0,16},{8,24},{16,0},{24,8},{32,48},{40,56},{48,32},{56,40},{64,80... | collective-permute-start | bytes 2359304 | tf_op jit(solution)/shard_map/ppermute | solution.py:179
  12.0 4.5 %collective-permute-start.4 = (bf16[384,512]{1,0:T(8,128)(2,1)}, bf16[384,512]{1,0:T(8,128)(2,1)}, u32[]{:S(2)}, u32[]{:S(2)}) collective-permute-start(bf16[384,512]{1,0:T(8,128)(2,1)} %fusion), channel_id=1, source_target_pairs={{0,32},{8,40},{16,48},{24,56},{32,0},{40,8},{48,16},{56,24},{64,96... | collective-permute-start | bytes 1179656 | tf_op jit(solution)/shard_map/ppermute | solution.py:179
  16.5 5.9 %collective-permute-start.5 = (bf16[384,512]{1,0:T(8,128)(2,1)}, bf16[384,512]{1,0:T(8,128)(2,1)}, u32[]{:S(2)}, u32[]{:S(2)}) collective-permute-start(bf16[384,512]{1,0:T(8,128)(2,1)} %param.7), channel_id=1, source_target_pairs={{0,64},{8,72},{16,80},{24,88},{32,96},{40,104},{48,112},{56,120},{... | collective-permute-start | bytes 1179656 | tf_op jit(solution)/shard_map/ppermute | solution.py:179
  22.5 0.8 copy.7
  23.3 0.1 reshape.10
  23.4 0.1 concatenate.6.scal
  23.5 0.0 copy-done
  23.5 1.8 %attend_own.1 = (f32[384,512]{1,0:T(8,128)S(1)}, f32[384,512]{1,0:T(8,128)S(1)}, f32[384,512]{1,0:T(8,128)S(1)}) custom-call(s32[58]{0:T(128)S(1)} %concatenate.6.scal, bf16[384,512]{1,0:T(8,128)(2,1)S(1)} %copy-done, bf16[384,1024]{1,0:T(8,128)(2,1)S(1)} %pad_maximum_fusion.1.refs_0_), custom_call_target="tpu_custom_call" | custom-call | flops 301989888 | bytes 1179648 | tf_op jit(solution)/shard_map/attend_own/pallas_call | solution.py:154
  25.3 0.1 pad_maximum_fusion
  25.4 5.0 %all_to_all.5.refs_2_ = bf16[2,384,1024]{2,1,0:T(8,128)(2,1)S(1)} all-to-all(bf16[2,384,1024]{2,1,0:T(8,128)(2,1)S(1)} %pad_maximum_fusion), channel_id=1, replica_groups=mesh['b5'=2,'b4'=2,'b3'=2,'b2'=2,'b1'=2,'b0'=2,'space'=8] {'b0'}, dimensions={0} | all-to-all | bytes 3145728 | tf_op jit(solution)/shard_map/all_to_all | solution.py:213
  30.4 9.5 %collective-permute-done.refs_0_ = bf16[384,1024]{1,0:T(8,128)(2,1)S(1)} collective-permute-done((bf16[384,1024]{1,0:T(8,128)(2,1)S(1)}, bf16[384,1024]{1,0:T(8,128)(2,1)S(1)}, u32[]{:S(2)}, u32[]{:S(2)}) %collective-permute-start) | collective-permute-done | bytes 786464 | tf_op jit(solution)/shard_map/ppermute | solution.py:179
  40.0 3.0 %collective-permute-done.1.refs_1_ = bf16[384,1024]{1,0:T(8,128)(2,1)S(1)} collective-permute-done((bf16[384,1024]{1,0:T(8,128)(2,1)S(1)}, bf16[384,1024]{1,0:T(8,128)(2,1)S(1)}, u32[]{:S(2)}, u32[]{:S(2)}) %collective-permute-start.1) | collective-permute-done | bytes 786464 | tf_op jit(solution)/shard_map/ppermute | solution.py:179
  42.9 3.5 %collective-permute-start.2 = (bf16[384,1024]{1,0:T(8,128)(2,1)S(1)}, bf16[384,1024]{1,0:T(8,128)(2,1)S(1)}, u32[]{:S(2)}, u32[]{:S(2)}) collective-permute-start(bf16[384,1024]{1,0:T(8,128)(2,1)S(1)} %pad_maximum_fusion.1.refs_0_), channel_id=1, source_target_pairs={{1,0},{2,1},{3,2},{4,3},{5,4},{6,5},{7,6},{9,8},{10,9},{11,10},{12... | collective-permute-start | bytes 2359304 | tf_op jit(solution)/shard_map/ppermute | solution.py:218
  46.4 2.4 %collective-permute-start.3 = (bf16[384,1024]{1,0:T(8,128)(2,1)S(1)}, bf16[384,1024]{1,0:T(8,128)(2,1)S(1)}, u32[]{:S(2)}, u32[]{:S(2)}) collective-permute-start(bf16[384,1024]{1,0:T(8,128)(2,1)S(1)} %pad_maximum_fusion.1.refs_0_), channel_id=1, source_target_pairs={{0,1},{1,2},{2,3},{3,4},{4,5},{5,6},{6,7},{8,9},{9,10},{10,11},{11... | collective-permute-start | bytes 2359304 | tf_op jit(solution)/shard_map/ppermute | solution.py:217
  48.8 0.0 collective-permute-done.4.refs_0_
  48.8 5.3 %collective-permute-start.7 = (bf16[384,512]{1,0:T(8,128)(2,1)}, bf16[384,512]{1,0:T(8,128)(2,1)S(1)}, u32[]{:S(2)}, u32[]{:S(2)}) collective-permute-start(bf16[384,512]{1,0:T(8,128)(2,1)} %collective-permute-done.4.refs_0_), channel_id=1, source_target_pairs={{0,96},{8,104},{16,112},{24,120},{32,64},{40,72},{48,80},{56,88},{... | collective-permute-start | bytes 1179656 | tf_op jit(solution)/shard_map/ppermute | solution.py:179
  54.1 7.7 %collective-permute-done.5.refs_1_ = bf16[384,512]{1,0:T(8,128)(2,1)} collective-permute-done((bf16[384,512]{1,0:T(8,128)(2,1)}, bf16[384,512]{1,0:T(8,128)(2,1)}, u32[]{:S(2)}, u32[]{:S(2)}) %collective-permute-start.5) | collective-permute-done | bytes 393248 | tf_op jit(solution)/shard_map/ppermute | solution.py:179
  61.8 1.9 %collective-permute-start.6 = (bf16[384,512]{1,0:T(8,128)(2,1)}, bf16[384,512]{1,0:T(8,128)(2,1)S(1)}, u32[]{:S(2)}, u32[]{:S(2)}) collective-permute-start(bf16[384,512]{1,0:T(8,128)(2,1)} %param.7), channel_id=1, source_target_pairs={{0,32},{8,40},{16,48},{24,56},{32,0},{40,8},{48,16},{56,24},{64,96... | collective-permute-start | bytes 1179656 | tf_op jit(solution)/shard_map/ppermute | solution.py:179
  63.7 3.3 %attend_5_4_0.1 = (f32[384,512]{1,0:T(8,128)S(1)}, f32[384,512]{1,0:T(8,128)S(1)}, f32[384,512]{1,0:T(8,128)S(1)}) custom-call(s32[58]{0:T(128)S(1)} %concatenate.6.scal, bf16[384,512]{1,0:T(8,128)(2,1)S(1)} %copy-done, bf16[384,1024]{1,0:T(8,128)(2,1)S(1)} %collective-permute-done.refs_0_, bf16[384,1024]{1,0:T(8,128)(2,1)S(1)} %collective-permute-done.1.refs_1_, ...), custom_call_target="tpu_custom_call" | custom-call | flops 905969664 | bytes 3145728 | tf_op jit(solution)/shard_map/attend_5_4_0/pallas_call | solution.py:154
  67.0 0.0 collective-permute-done.8.refs_0_
  67.1 1.9 %attend_1.1 = (f32[384,512]{1,0:T(8,128)S(1)}, f32[384,512]{1,0:T(8,128)S(1)}, f32[384,512]{1,0:T(8,128)S(1)}) custom-call(s32[58]{0:T(128)S(1)} %concatenate.6.scal, bf16[384,512]{1,0:T(8,128)(2,1)S(1)} %copy-done, bf16[384,1024]{1,0:T(8,128)(2,1)S(1)} %collective-permute-done.8.refs_0_, f32[384,512]{1,0:T(8,128)S(1)} %get-tuple-element.31.refs_1_, ...), custom_call_target="tpu_custom_call" | custom-call | flops 301989888 | bytes 2359296 | tf_op jit(solution)/shard_map/attend_1/pallas_call | solution.py:154
  69.0 3.3 %collective-permute-done.7.refs_0_ = bf16[384,512]{1,0:T(8,128)(2,1)S(1)} collective-permute-done((bf16[384,512]{1,0:T(8,128)(2,1)}, bf16[384,512]{1,0:T(8,128)(2,1)S(1)}, u32[]{:S(2)}, u32[]{:S(2)}) %collective-permute-start.7) | collective-permute-done | bytes 393248 | tf_op jit(solution)/shard_map/ppermute | solution.py:179
  72.2 2.3 %attend_3.1 = (f32[384,512]{1,0:T(8,128)S(1)}, f32[384,512]{1,0:T(8,128)S(1)}, f32[384,512]{1,0:T(8,128)S(1)}) custom-call(s32[58]{0:T(128)S(1)} %concatenate.6.scal, bf16[384,512]{1,0:T(8,128)(2,1)S(1)} %copy-done, bf16[384,512]{1,0:T(8,128)(2,1)S(1)} %collective-permute-done.7.refs_0_, bf16[384,512]{1,0:T(8,128)(2,1)} %collective-permute-done.5.refs_1_, ...), custom_call_target="tpu_custom_call" | custom-call | flops 301989888 | bytes 2752512 | tf_op jit(solution)/shard_map/attend_3/pallas_call | solution.py:154
  74.6 5.6 %collective-permute-done.6.refs_1_ = bf16[384,512]{1,0:T(8,128)(2,1)S(1)} collective-permute-done((bf16[384,512]{1,0:T(8,128)(2,1)}, bf16[384,512]{1,0:T(8,128)(2,1)S(1)}, u32[]{:S(2)}, u32[]{:S(2)}) %collective-permute-start.6) | collective-permute-done | bytes 393248 | tf_op jit(solution)/shard_map/ppermute | solution.py:179
  80.2 2.3 %attend_2.1 = (f32[384,512]{1,0:T(8,128)S(1)}, f32[384,512]{1,0:T(8,128)S(1)}, f32[384,512]{1,0:T(8,128)S(1)}) custom-call(s32[58]{0:T(128)S(1)} %concatenate.6.scal, bf16[384,512]{1,0:T(8,128)(2,1)S(1)} %copy-done, bf16[384,512]{1,0:T(8,128)(2,1)} %collective-permute-done.4.refs_0_, bf16[384,512]{1,0:T(8,128)(2,1)S(1)} %collective-permute-done.6.refs_1_, ...), custom_call_target="tpu_custom_call" | custom-call | flops 301989888 | bytes 2752512 | tf_op jit(solution)/shard_map/attend_2/pallas_call | solution.py:154
  82.5 0.0 collective-permute-done.2.refs_0_
  82.5 6.6 %collective-permute-done.3.refs_1_ = bf16[384,1024]{1,0:T(8,128)(2,1)S(1)} collective-permute-done((bf16[384,1024]{1,0:T(8,128)(2,1)S(1)}, bf16[384,1024]{1,0:T(8,128)(2,1)S(1)}, u32[]{:S(2)}, u32[]{:S(2)}) %collective-permute-start.3) | collective-permute-done | bytes 786464 | tf_op jit(solution)/shard_map/ppermute | solution.py:217
  89.2 3.2 %attend_high_low.1 = bf16[384,512]{1,0:T(8,128)(2,1)} custom-call(s32[58]{0:T(128)S(1)} %concatenate.6.scal, bf16[384,512]{1,0:T(8,128)(2,1)S(1)} %copy-done, bf16[384,1024]{1,0:T(8,128)(2,1)S(1)} %collective-permute-done.2.refs_0_, bf16[384,1024]{1,0:T(8,128)(2,1)S(1)} %collective-permute-done.3.refs_1_, f32[384,512]{1,0:T(8,128)S(1)} %get-tuple-element.40.refs_2_, ...), custom_call_target="tpu_custom_call" | custom-call | flops 603979776 | bytes 2752512 | tf_op jit(solution)/shard_map/attend_high_low/pallas_call | solution.py:154
  (4 shorter events, 0.0 us)
Async XLA Ops:
  0.0 23.5 %copy-start = (bf16[384,512]{1,0:T(8,128)(2,1)S(1)}, bf16[384,512]{1,0:T(8,128)(2,1)}, u32[]{:S(2)}) copy-start(bf16[384,512]{1,0:T(8,128)(2,1)} %q_ref.11) | copy-start | bytes 1179652
  3.8 36.1 %collective-permute-start = (bf16[384,1024]{1,0:T(8,128)(2,1)S(1)}, bf16[384,1024]{1,0:T(8,128)(2,1)S(1)}, u32[]{:S(2)}, u32[]{:S(2)}) collective-permute-start(bf16[384,1024]{1,0:T(8,128)(2,1)S(1)} %pad_maximum_fusion.1.refs_0_), channel_id=1, source_target_pairs={{0,256},{8,264},{16,272},{24,280},{32,288},{40,296},{48,304},{56,3... | collective-permute-start | bytes 2359304 | tf_op jit(solution)/shard_map/ppermute | solution.py:179
  6.3 36.6 %collective-permute-start.1 = (bf16[384,1024]{1,0:T(8,128)(2,1)S(1)}, bf16[384,1024]{1,0:T(8,128)(2,1)S(1)}, u32[]{:S(2)}, u32[]{:S(2)}) collective-permute-start(bf16[384,1024]{1,0:T(8,128)(2,1)S(1)} %pad_maximum_fusion.1.refs_0_), channel_id=1, source_target_pairs={{0,128},{8,136},{16,144},{24,152},{32,160},{40,168},{48,176},{56,1... | collective-permute-start | bytes 2359304 | tf_op jit(solution)/shard_map/ppermute | solution.py:179
  9.7 57.4 %collective-permute-start.8 = (bf16[384,1024]{1,0:T(8,128)(2,1)S(1)}, bf16[384,1024]{1,0:T(8,128)(2,1)S(1)}, u32[]{:S(2)}, u32[]{:S(2)}) collective-permute-start(bf16[384,1024]{1,0:T(8,128)(2,1)S(1)} %pad_maximum_fusion.1.refs_0_), channel_id=1, source_target_pairs={{0,16},{8,24},{16,0},{24,8},{32,48},{40,56},{48,32},{56,40},{64,80... | collective-permute-start | bytes 2359304 | tf_op jit(solution)/shard_map/ppermute | solution.py:179
  12.0 36.7 %collective-permute-start.4 = (bf16[384,512]{1,0:T(8,128)(2,1)}, bf16[384,512]{1,0:T(8,128)(2,1)}, u32[]{:S(2)}, u32[]{:S(2)}) collective-permute-start(bf16[384,512]{1,0:T(8,128)(2,1)} %fusion), channel_id=1, source_target_pairs={{0,32},{8,40},{16,48},{24,56},{32,0},{40,8},{48,16},{56,24},{64,96... | collective-permute-start | bytes 1179656 | tf_op jit(solution)/shard_map/ppermute | solution.py:179
  16.5 45.2 %collective-permute-start.5 = (bf16[384,512]{1,0:T(8,128)(2,1)}, bf16[384,512]{1,0:T(8,128)(2,1)}, u32[]{:S(2)}, u32[]{:S(2)}) collective-permute-start(bf16[384,512]{1,0:T(8,128)(2,1)} %param.7), channel_id=1, source_target_pairs={{0,64},{8,72},{16,80},{24,88},{32,96},{40,104},{48,112},{56,120},{... | collective-permute-start | bytes 1179656 | tf_op jit(solution)/shard_map/ppermute | solution.py:179
  42.9 39.6 %collective-permute-start.2 = (bf16[384,1024]{1,0:T(8,128)(2,1)S(1)}, bf16[384,1024]{1,0:T(8,128)(2,1)S(1)}, u32[]{:S(2)}, u32[]{:S(2)}) collective-permute-start(bf16[384,1024]{1,0:T(8,128)(2,1)S(1)} %pad_maximum_fusion.1.refs_0_), channel_id=1, source_target_pairs={{1,0},{2,1},{3,2},{4,3},{5,4},{6,5},{7,6},{9,8},{10,9},{11,10},{12... | collective-permute-start | bytes 2359304 | tf_op jit(solution)/shard_map/ppermute | solution.py:218
  46.4 42.8 %collective-permute-start.3 = (bf16[384,1024]{1,0:T(8,128)(2,1)S(1)}, bf16[384,1024]{1,0:T(8,128)(2,1)S(1)}, u32[]{:S(2)}, u32[]{:S(2)}) collective-permute-start(bf16[384,1024]{1,0:T(8,128)(2,1)S(1)} %pad_maximum_fusion.1.refs_0_), channel_id=1, source_target_pairs={{0,1},{1,2},{2,3},{3,4},{4,5},{5,6},{6,7},{8,9},{9,10},{10,11},{11... | collective-permute-start | bytes 2359304 | tf_op jit(solution)/shard_map/ppermute | solution.py:217
  48.8 23.4 %collective-permute-start.7 = (bf16[384,512]{1,0:T(8,128)(2,1)}, bf16[384,512]{1,0:T(8,128)(2,1)S(1)}, u32[]{:S(2)}, u32[]{:S(2)}) collective-permute-start(bf16[384,512]{1,0:T(8,128)(2,1)} %collective-permute-done.4.refs_0_), channel_id=1, source_target_pairs={{0,96},{8,104},{16,112},{24,120},{32,64},{40,72},{48,80},{56,88},{... | collective-permute-start | bytes 1179656 | tf_op jit(solution)/shard_map/ppermute | solution.py:179
  61.8 18.4 %collective-permute-start.6 = (bf16[384,512]{1,0:T(8,128)(2,1)}, bf16[384,512]{1,0:T(8,128)(2,1)S(1)}, u32[]{:S(2)}, u32[]{:S(2)}) collective-permute-start(bf16[384,512]{1,0:T(8,128)(2,1)} %param.7), channel_id=1, source_target_pairs={{0,32},{8,40},{16,48},{24,56},{32,0},{40,8},{48,16},{56,24},{64,96... | collective-permute-start | bytes 1179656 | tf_op jit(solution)/shard_map/ppermute | solution.py:179

commit v6 on v5

--- a/solution.py
+++ b/solution.py
@@ -191,18 +191,20 @@
             block_mask.reshape(-1),
         ]
     )
-    column = lax.broadcasted_iota(jnp.int32, (rows, width), 1) // HEAD
-    row = lax.broadcasted_iota(jnp.int32, (rows, width), 0)
+    column = lax.broadcasted_iota(jnp.int32, (1, width), 1) // HEAD
     code = jnp.where(
         column == 0,
         jnp.float32(jnp.inf),
         jnp.where(column == 1, count >> 7, count & 127).astype(jnp.float32),
     ).astype(jnp.bfloat16)
-    marked = jnp.where((row == rows - 1) & (count < rows), code, keys)
+    end = jnp.where(count < rows, code, keys[rows - 1 :])
+    marked = lax.dynamic_update_slice(keys, end, (rows - 1, 0))
 
     up = [(i, i + 1) for i in range(space_size - 1)]
     down = [(i + 1, i) for i in range(space_size - 1)]
-    both = jnp.concatenate([marked, values], axis=1)
+    both = lax.dynamic_update_slice(
+        jnp.concatenate([keys, values], axis=1), end, (rows - 1, 0)
+    )
     y2_k = partner(marked, 4)
     y4_v = partner(values, 8)
     y1 = partner(both, 2)

time: 92.9 us -> 92.2 us (level)
  waiting for transfers between devices: 35.7 us -> 26.9 us
  starting transfers between devices: 31.6 us -> 38.9 us
  local copies, waits for them, and re-layouts: 0.97 us -> 3.62 us
  other arithmetic: 3.24 us -> 1.23 us
    ppermute x7, waiting for transfers between devices: 29.1 us -> 20.6 us  [partner(): return lax.ppermute(value, TM, [(i, i ^ mask) for i in range(tm_size)])]
    ppermute x7, starting transfers between devices: 25.8 us -> 33.1 us  [partner(): return lax.ppermute(value, TM, [(i, i ^ mask) for i in range(tm_size)])]
    select_n x1, other arithmetic: 1.89 us -> 0.01 us  [per_device(): end = jnp.where(count < rows, code, keys[rows - 1:])]
    dynamic_update_slice x0 -> x2, local copies, waits for them, and re-layouts: none -> 1.59 us  [the longest x1 1.32 us: per_device(): marked = lax.dynamic_update_slice(keys, end, (rows - 1, 0))]
    unnamed x3 -> x8, local copies, waits for them, and re-layouts: 0.8 us -> 1.85 us
  transfers between devices with their start and end apart: 9 -> 9, of which waited for: 6 -> 7; matrix products, arithmetic and copies ran while one was open for 1% -> 3% of each run, Pallas kernels for 13% -> 13%
where the time goes in v6:
time: 92.2 us; the launch traced here: 91.6 us
  starting transfers between devices  38.9 us (42%)
  waiting for transfers between devices  26.9 us (29%)
  Pallas kernels  14.9 us (16%)
  blocking collectives  5.13 us (6%)
  local copies, waits for them, and re-layouts  3.62 us (4%)
  other arithmetic  1.23 us (1%)
    ppermute x7, starting transfers between devices, partner(): return lax.ppermute(value, TM, [(i, i ^ mask) for i in range(tm_size)])  33.1 us
    ppermute x7, waiting for transfers between devices, partner(): return lax.ppermute(value, TM, [(i, i ^ mask) for i in range(tm_size)])  20.6 us
    pallas_call x6, Pallas kernels, attend(): pl.pallas_call(functools.partial(attend_kernel, kinds, packed, first, las...  14.9 us
    ppermute x1, waiting for transfers between devices, per_device(): low = lax.ppermute(second, 'space', up)  6.34 us
    all_to_all x1, blocking collectives, per_device(): core = lax.all_to_all(jnp.stack([own, own]), 'b0', 0, 0)  5.13 us
    ppermute x1, starting transfers between devices, per_device(): high = lax.ppermute(second, 'space', down)  3.46 us
    ppermute x1, starting transfers between devices, per_device(): low = lax.ppermute(second, 'space', up)  2.37 us
    unnamed x8, local copies, waits for them, and re-layouts  1.85 us
  transfers between devices with their start and end apart: 9, of which 7 were waited for; matrix products, arithmetic and copies ran while one was open for 3% of the time, Pallas kernels for 13%

profile of v6, /device:TPU:392, one launch (start us, length us, event | category | flops | bytes accessed | tf_op | source)
XLA Modules:
  0.0 91.6 jit_solution(4300265084116256459)
XLA Ops:
  0.0 1.0 %copy.12 = bf16[384,512]{1,0:T(8,128)(2,1)S(1)} copy(bf16[384,512]{1,0:T(8,128)(2,1)} %param.6) | data formatting | bytes 786432
  1.7 1.1 %pad_maximum_fusion.1 = bf16[384,1024]{1,0:T(8,128)(2,1)S(1)} fusion(bf16[384,512]{1,0:T(8,128)(2,1)} %param.7, bf16[384,512]{1,0:T(8,128)(2,1)S(1)} %copy.12), kind=kLoop, calls=%fused_computation.1 | loop fusion | flops 1572864 | bytes 1572864 | tf_op jit(solution)/shard_map/concatenate | solution.py:206
  2.8 0.3 dynamic_update_slice.6.refs_0_
  3.1 2.5 %collective-permute-start = (bf16[384,1024]{1,0:T(8,128)(2,1)S(1)}, bf16[384,1024]{1,0:T(8,128)(2,1)S(1)}, u32[]{:S(2)}, u32[]{:S(2)}) collective-permute-start(bf16[384,1024]{1,0:T(8,128)(2,1)S(1)} %dynamic_update_slice.6.refs_0_), channel_id=1, source_target_pairs={{0,256},{8,264},{16,272},{24,280},{32,288},{40,296},{48,304},{56,3... | collective-permute-start | bytes 2359304 | tf_op jit(solution)/shard_map/ppermute | solution.py:179
  5.6 3.4 %collective-permute-start.1 = (bf16[384,1024]{1,0:T(8,128)(2,1)S(1)}, bf16[384,1024]{1,0:T(8,128)(2,1)S(1)}, u32[]{:S(2)}, u32[]{:S(2)}) collective-permute-start(bf16[384,1024]{1,0:T(8,128)(2,1)S(1)} %dynamic_update_slice.6.refs_0_), channel_id=1, source_target_pairs={{0,128},{8,136},{16,144},{24,152},{32,160},{40,168},{48,176},{56,1... | collective-permute-start | bytes 2359304 | tf_op jit(solution)/shard_map/ppermute | solution.py:179
  8.9 2.4 %collective-permute-start.8 = (bf16[384,1024]{1,0:T(8,128)(2,1)S(1)}, bf16[384,1024]{1,0:T(8,128)(2,1)S(1)}, u32[]{:S(2)}, u32[]{:S(2)}) collective-permute-start(bf16[384,1024]{1,0:T(8,128)(2,1)S(1)} %dynamic_update_slice.6.refs_0_), channel_id=1, source_target_pairs={{0,16},{8,24},{16,0},{24,8},{32,48},{40,56},{48,32},{56,40},{64,80... | collective-permute-start | bytes 2359304 | tf_op jit(solution)/shard_map/ppermute | solution.py:179
  11.3 7.7 %collective-permute-start.5 = (bf16[384,512]{1,0:T(8,128)(2,1)}, bf16[384,512]{1,0:T(8,128)(2,1)}, u32[]{:S(2)}, u32[]{:S(2)}) collective-permute-start(bf16[384,512]{1,0:T(8,128)(2,1)} %param.7), channel_id=1, source_target_pairs={{0,64},{8,72},{16,80},{24,88},{32,96},{40,104},{48,112},{56,120},{... | collective-permute-start | bytes 1179656 | tf_op jit(solution)/shard_map/ppermute | solution.py:179
  19.1 1.3 %dynamic_update_slice.7 = bf16[384,512]{1,0:T(8,128)(2,1)} dynamic-update-slice(bf16[384,512]{1,0:T(8,128)(2,1)} %copy-done.1, bf16[1,512]{1,0:T(2,128)(2,1)S(1)} %broadcast_select_fusion, s32[]{:T(128)} %constant.43.clone.1, s32[]{:T(128)} %constant.32.clone.1) | dynamic-update-slice | bytes 2052 | tf_op jit(solution)/shard_map/dynamic_update_slice | solution.py:201
  20.4 2.7 %collective-permute-start.4 = (bf16[384,512]{1,0:T(8,128)(2,1)}, bf16[384,512]{1,0:T(8,128)(2,1)}, u32[]{:S(2)}, u32[]{:S(2)}) collective-permute-start(bf16[384,512]{1,0:T(8,128)(2,1)} %dynamic_update_slice.7), channel_id=1, source_target_pairs={{0,32},{8,40},{16,48},{24,56},{32,0},{40,8},{48,16},{56,24},{64,96... | collective-permute-start | bytes 1179656 | tf_op jit(solution)/shard_map/ppermute | solution.py:179
  23.1 0.8 copy.7
  23.9 0.1 reshape.92
  24.0 0.1 concatenate.6.scal
  24.1 1.8 %attend_own.1 = (f32[384,512]{1,0:T(8,128)S(1)}, f32[384,512]{1,0:T(8,128)S(1)}, f32[384,512]{1,0:T(8,128)S(1)}) custom-call(s32[58]{0:T(128)S(1)} %concatenate.6.scal, bf16[384,512]{1,0:T(8,128)(2,1)S(1)} %copy-done, bf16[384,1024]{1,0:T(8,128)(2,1)S(1)} %dynamic_update_slice.6.refs_0_), custom_call_target="tpu_custom_call" | custom-call | flops 301989888 | bytes 1179648 | tf_op jit(solution)/shard_map/attend_own/pallas_call | solution.py:154
  25.9 0.1 pad_maximum_fusion
  26.0 0.0 copy-start.2
  26.0 5.1 %all_to_all.5.refs_2_ = bf16[2,384,1024]{2,1,0:T(8,128)(2,1)S(1)} all-to-all(bf16[2,384,1024]{2,1,0:T(8,128)(2,1)S(1)} %pad_maximum_fusion), channel_id=1, replica_groups=mesh['b5'=2,'b4'=2,'b3'=2,'b2'=2,'b1'=2,'b0'=2,'space'=8] {'b0'}, dimensions={0} | all-to-all | bytes 3145728 | tf_op jit(solution)/shard_map/all_to_all | solution.py:215
  31.2 8.1 %collective-permute-done.refs_0_ = bf16[384,1024]{1,0:T(8,128)(2,1)S(1)} collective-permute-done((bf16[384,1024]{1,0:T(8,128)(2,1)S(1)}, bf16[384,1024]{1,0:T(8,128)(2,1)S(1)}, u32[]{:S(2)}, u32[]{:S(2)}) %collective-permute-start) | collective-permute-done | bytes 786464 | tf_op jit(solution)/shard_map/ppermute | solution.py:179
  39.2 3.0 %collective-permute-done.1.refs_1_ = bf16[384,1024]{1,0:T(8,128)(2,1)S(1)} collective-permute-done((bf16[384,1024]{1,0:T(8,128)(2,1)S(1)}, bf16[384,1024]{1,0:T(8,128)(2,1)S(1)}, u32[]{:S(2)}, u32[]{:S(2)}) %collective-permute-start.1) | collective-permute-done | bytes 786464 | tf_op jit(solution)/shard_map/ppermute | solution.py:179
  42.2 3.5 %collective-permute-start.2 = (bf16[384,1024]{1,0:T(8,128)(2,1)S(1)}, bf16[384,1024]{1,0:T(8,128)(2,1)S(1)}, u32[]{:S(2)}, u32[]{:S(2)}) collective-permute-start(bf16[384,1024]{1,0:T(8,128)(2,1)S(1)} %dynamic_update_slice.6.refs_0_), channel_id=1, source_target_pairs={{1,0},{2,1},{3,2},{4,3},{5,4},{6,5},{7,6},{9,8},{10,9},{11,10},{12... | collective-permute-start | bytes 2359304 | tf_op jit(solution)/shard_map/ppermute | solution.py:220
  45.7 2.4 %collective-permute-start.3 = (bf16[384,1024]{1,0:T(8,128)(2,1)S(1)}, bf16[384,1024]{1,0:T(8,128)(2,1)S(1)}, u32[]{:S(2)}, u32[]{:S(2)}) collective-permute-start(bf16[384,1024]{1,0:T(8,128)(2,1)S(1)} %dynamic_update_slice.6.refs_0_), channel_id=1, source_target_pairs={{0,1},{1,2},{2,3},{3,4},{4,5},{5,6},{6,7},{8,9},{9,10},{10,11},{11... | collective-permute-start | bytes 2359304 | tf_op jit(solution)/shard_map/ppermute | solution.py:219
  48.0 0.3 collective-permute-done.4.refs_0_
  48.4 10.9 %collective-permute-start.7 = (bf16[384,512]{1,0:T(8,128)(2,1)}, bf16[384,512]{1,0:T(8,128)(2,1)S(1)}, u32[]{:S(2)}, u32[]{:S(2)}) collective-permute-start(bf16[384,512]{1,0:T(8,128)(2,1)} %collective-permute-done.4.refs_0_), channel_id=1, source_target_pairs={{0,96},{8,104},{16,112},{24,120},{32,64},{40,72},{48,80},{56,88},{... | collective-permute-start | bytes 1179656 | tf_op jit(solution)/shard_map/ppermute | solution.py:179
  59.3 1.7 %collective-permute-done.5.refs_1_ = bf16[384,512]{1,0:T(8,128)(2,1)} collective-permute-done((bf16[384,512]{1,0:T(8,128)(2,1)}, bf16[384,512]{1,0:T(8,128)(2,1)}, u32[]{:S(2)}, u32[]{:S(2)}) %collective-permute-start.5) | collective-permute-done | bytes 393248 | tf_op jit(solution)/shard_map/ppermute | solution.py:179
  61.1 3.5 %collective-permute-start.6 = (bf16[384,512]{1,0:T(8,128)(2,1)S(1)}, bf16[384,512]{1,0:T(8,128)(2,1)S(1)}, u32[]{:S(2)}, u32[]{:S(2)}) collective-permute-start(bf16[384,512]{1,0:T(8,128)(2,1)S(1)} %copy-done.2), channel_id=1, source_target_pairs={{0,32},{8,40},{16,48},{24,56},{32,0},{40,8},{48,16},{56,24},{64,96... | collective-permute-start | bytes 1179656 | tf_op jit(solution)/shard_map/ppermute | solution.py:179
  64.6 3.3 %attend_5_4_0.1 = (f32[384,512]{1,0:T(8,128)S(1)}, f32[384,512]{1,0:T(8,128)S(1)}, f32[384,512]{1,0:T(8,128)S(1)}) custom-call(s32[58]{0:T(128)S(1)} %concatenate.6.scal, bf16[384,512]{1,0:T(8,128)(2,1)S(1)} %copy-done, bf16[384,1024]{1,0:T(8,128)(2,1)S(1)} %collective-permute-done.refs_0_, bf16[384,1024]{1,0:T(8,128)(2,1)S(1)} %collective-permute-done.1.refs_1_, ...), custom_call_target="tpu_custom_call" | custom-call | flops 905969664 | bytes 3145728 | tf_op jit(solution)/shard_map/attend_5_4_0/pallas_call | solution.py:154
  68.0 1.9 %attend_1.1 = (f32[384,512]{1,0:T(8,128)S(1)}, f32[384,512]{1,0:T(8,128)S(1)}, f32[384,512]{1,0:T(8,128)S(1)}) custom-call(s32[58]{0:T(128)S(1)} %concatenate.6.scal, bf16[384,512]{1,0:T(8,128)(2,1)S(1)} %copy-done, bf16[384,1024]{1,0:T(8,128)(2,1)S(1)} %collective-permute-done.8.refs_0_, f32[384,512]{1,0:T(8,128)S(1)} %get-tuple-element.31.refs_1_, ...), custom_call_target="tpu_custom_call" | custom-call | flops 301989888 | bytes 2359296 | tf_op jit(solution)/shard_map/attend_1/pallas_call | solution.py:154
  69.9 4.1 %collective-permute-done.7.refs_0_ = bf16[384,512]{1,0:T(8,128)(2,1)S(1)} collective-permute-done((bf16[384,512]{1,0:T(8,128)(2,1)}, bf16[384,512]{1,0:T(8,128)(2,1)S(1)}, u32[]{:S(2)}, u32[]{:S(2)}) %collective-permute-start.7) | collective-permute-done | bytes 393248 | tf_op jit(solution)/shard_map/ppermute | solution.py:179
  74.0 2.3 %attend_3.1 = (f32[384,512]{1,0:T(8,128)S(1)}, f32[384,512]{1,0:T(8,128)S(1)}, f32[384,512]{1,0:T(8,128)S(1)}) custom-call(s32[58]{0:T(128)S(1)} %concatenate.6.scal, bf16[384,512]{1,0:T(8,128)(2,1)S(1)} %copy-done, bf16[384,512]{1,0:T(8,128)(2,1)S(1)} %collective-permute-done.7.refs_0_, bf16[384,512]{1,0:T(8,128)(2,1)} %collective-permute-done.5.refs_1_, ...), custom_call_target="tpu_custom_call" | custom-call | flops 301989888 | bytes 2752512 | tf_op jit(solution)/shard_map/attend_3/pallas_call | solution.py:154
  76.3 3.4 %collective-permute-done.6.refs_1_ = bf16[384,512]{1,0:T(8,128)(2,1)S(1)} collective-permute-done((bf16[384,512]{1,0:T(8,128)(2,1)S(1)}, bf16[384,512]{1,0:T(8,128)(2,1)S(1)}, u32[]{:S(2)}, u32[]{:S(2)}) %collective-permute-start.6) | collective-permute-done | bytes 393248 | tf_op jit(solution)/shard_map/ppermute | solution.py:179
  79.7 2.3 %attend_2.1 = (f32[384,512]{1,0:T(8,128)S(1)}, f32[384,512]{1,0:T(8,128)S(1)}, f32[384,512]{1,0:T(8,128)S(1)}) custom-call(s32[58]{0:T(128)S(1)} %concatenate.6.scal, bf16[384,512]{1,0:T(8,128)(2,1)S(1)} %copy-done, bf16[384,512]{1,0:T(8,128)(2,1)} %collective-permute-done.4.refs_0_, bf16[384,512]{1,0:T(8,128)(2,1)S(1)} %collective-permute-done.6.refs_1_, ...), custom_call_target="tpu_custom_call" | custom-call | flops 301989888 | bytes 2752512 | tf_op jit(solution)/shard_map/attend_2/pallas_call | solution.py:154
  82.1 6.3 %collective-permute-done.3.refs_1_ = bf16[384,1024]{1,0:T(8,128)(2,1)S(1)} collective-permute-done((bf16[384,1024]{1,0:T(8,128)(2,1)S(1)}, bf16[384,1024]{1,0:T(8,128)(2,1)S(1)}, u32[]{:S(2)}, u32[]{:S(2)}) %collective-permute-start.3) | collective-permute-done | bytes 786464 | tf_op jit(solution)/shard_map/ppermute | solution.py:219
  88.4 3.2 %attend_high_low.1 = bf16[384,512]{1,0:T(8,128)(2,1)} custom-call(s32[58]{0:T(128)S(1)} %concatenate.6.scal, bf16[384,512]{1,0:T(8,128)(2,1)S(1)} %copy-done, bf16[384,1024]{1,0:T(8,128)(2,1)S(1)} %collective-permute-done.2.refs_0_, bf16[384,1024]{1,0:T(8,128)(2,1)S(1)} %collective-permute-done.3.refs_1_, f32[384,512]{1,0:T(8,128)S(1)} %get-tuple-element.40.refs_2_, ...), custom_call_target="tpu_custom_call" | custom-call | flops 603979776 | bytes 2752512 | tf_op jit(solution)/shard_map/attend_high_low/pallas_call | solution.py:154
  (8 shorter events, 0.0 us)
Async XLA Ops:
  0.0 24.1 %copy-start = (bf16[384,512]{1,0:T(8,128)(2,1)S(1)}, bf16[384,512]{1,0:T(8,128)(2,1)}, u32[]{:S(2)}) copy-start(bf16[384,512]{1,0:T(8,128)(2,1)} %q_ref.11) | copy-start | bytes 1179652
  1.1 1.7 %copy-start.1 = (bf16[384,512]{1,0:T(8,128)(2,1)}, bf16[384,512]{1,0:T(8,128)(2,1)S(1)}, u32[]{:S(2)}) copy-start(bf16[384,512]{1,0:T(8,128)(2,1)S(1)} %copy.12) | copy-start | bytes 1179652
  3.1 36.1 %collective-permute-start = (bf16[384,1024]{1,0:T(8,128)(2,1)S(1)}, bf16[384,1024]{1,0:T(8,128)(2,1)S(1)}, u32[]{:S(2)}, u32[]{:S(2)}) collective-permute-start(bf16[384,1024]{1,0:T(8,128)(2,1)S(1)} %dynamic_update_slice.6.refs_0_), channel_id=1, source_target_pairs={{0,256},{8,264},{16,272},{24,280},{32,288},{40,296},{48,304},{56,3... | collective-permute-start | bytes 2359304 | tf_op jit(solution)/shard_map/ppermute | solution.py:179
  5.6 36.6 %collective-permute-start.1 = (bf16[384,1024]{1,0:T(8,128)(2,1)S(1)}, bf16[384,1024]{1,0:T(8,128)(2,1)S(1)}, u32[]{:S(2)}, u32[]{:S(2)}) collective-permute-start(bf16[384,1024]{1,0:T(8,128)(2,1)S(1)} %dynamic_update_slice.6.refs_0_), channel_id=1, source_target_pairs={{0,128},{8,136},{16,144},{24,152},{32,160},{40,168},{48,176},{56,1... | collective-permute-start | bytes 2359304 | tf_op jit(solution)/shard_map/ppermute | solution.py:179
  8.9 59.0 %collective-permute-start.8 = (bf16[384,1024]{1,0:T(8,128)(2,1)S(1)}, bf16[384,1024]{1,0:T(8,128)(2,1)S(1)}, u32[]{:S(2)}, u32[]{:S(2)}) collective-permute-start(bf16[384,1024]{1,0:T(8,128)(2,1)S(1)} %dynamic_update_slice.6.refs_0_), channel_id=1, source_target_pairs={{0,16},{8,24},{16,0},{24,8},{32,48},{40,56},{48,32},{56,40},{64,80... | collective-permute-start | bytes 2359304 | tf_op jit(solution)/shard_map/ppermute | solution.py:179
  11.3 49.7 %collective-permute-start.5 = (bf16[384,512]{1,0:T(8,128)(2,1)}, bf16[384,512]{1,0:T(8,128)(2,1)}, u32[]{:S(2)}, u32[]{:S(2)}) collective-permute-start(bf16[384,512]{1,0:T(8,128)(2,1)} %param.7), channel_id=1, source_target_pairs={{0,64},{8,72},{16,80},{24,88},{32,96},{40,104},{48,112},{56,120},{... | collective-permute-start | bytes 1179656 | tf_op jit(solution)/shard_map/ppermute | solution.py:179
  20.4 28.0 %collective-permute-start.4 = (bf16[384,512]{1,0:T(8,128)(2,1)}, bf16[384,512]{1,0:T(8,128)(2,1)}, u32[]{:S(2)}, u32[]{:S(2)}) collective-permute-start(bf16[384,512]{1,0:T(8,128)(2,1)} %dynamic_update_slice.7), channel_id=1, source_target_pairs={{0,32},{8,40},{16,48},{24,56},{32,0},{40,8},{48,16},{56,24},{64,96... | collective-permute-start | bytes 1179656 | tf_op jit(solution)/shard_map/ppermute | solution.py:179
  26.0 35.0 %copy-start.2 = (bf16[384,512]{1,0:T(8,128)(2,1)S(1)}, bf16[384,512]{1,0:T(8,128)(2,1)}, u32[]{:S(2)}) copy-start(bf16[384,512]{1,0:T(8,128)(2,1)} %param.7) | copy-start | bytes 1179652
  42.2 39.9 %collective-permute-start.2 = (bf16[384,1024]{1,0:T(8,128)(2,1)S(1)}, bf16[384,1024]{1,0:T(8,128)(2,1)S(1)}, u32[]{:S(2)}, u32[]{:S(2)}) collective-permute-start(bf16[384,1024]{1,0:T(8,128)(2,1)S(1)} %dynamic_update_slice.6.refs_0_), channel_id=1, source_target_pairs={{1,0},{2,1},{3,2},{4,3},{5,4},{6,5},{7,6},{9,8},{10,9},{11,10},{12... | collective-permute-start | bytes 2359304 | tf_op jit(solution)/shard_map/ppermute | solution.py:220
  45.7 42.8 %collective-permute-start.3 = (bf16[384,1024]{1,0:T(8,128)(2,1)S(1)}, bf16[384,1024]{1,0:T(8,128)(2,1)S(1)}, u32[]{:S(2)}, u32[]{:S(2)}) collective-permute-start(bf16[384,1024]{1,0:T(8,128)(2,1)S(1)} %dynamic_update_slice.6.refs_0_), channel_id=1, source_target_pairs={{0,1},{1,2},{2,3},{3,4},{4,5},{5,6},{6,7},{8,9},{9,10},{10,11},{11... | collective-permute-start | bytes 2359304 | tf_op jit(solution)/shard_map/ppermute | solution.py:219
  48.4 25.6 %collective-permute-start.7 = (bf16[384,512]{1,0:T(8,128)(2,1)}, bf16[384,512]{1,0:T(8,128)(2,1)S(1)}, u32[]{:S(2)}, u32[]{:S(2)}) collective-permute-start(bf16[384,512]{1,0:T(8,128)(2,1)} %collective-permute-done.4.refs_0_), channel_id=1, source_target_pairs={{0,96},{8,104},{16,112},{24,120},{32,64},{40,72},{48,80},{56,88},{... | collective-permute-start | bytes 1179656 | tf_op jit(solution)/shard_map/ppermute | solution.py:179
  61.1 18.7 %collective-permute-start.6 = (bf16[384,512]{1,0:T(8,128)(2,1)S(1)}, bf16[384,512]{1,0:T(8,128)(2,1)S(1)}, u32[]{:S(2)}, u32[]{:S(2)}) collective-permute-start(bf16[384,512]{1,0:T(8,128)(2,1)S(1)} %copy-done.2), channel_id=1, source_target_pairs={{0,32},{8,40},{16,48},{24,56},{32,0},{40,8},{48,16},{56,24},{64,96... | collective-permute-start | bytes 1179656 | tf_op jit(solution)/shard_map/ppermute | solution.py:179
